TPU v7x, 512 devices: a whole 4x4x16 slice. The times are simulated.
512 devices in a mesh: blk: 32 (over y, x, core), int: 16 (over z).
Axes of the slice: x: 4, y: 4, z: 16, core: 2. Of those that a mesh axis runs over, the one named last changes fastest.
Arguments:
- amplitudes: float32 [4, 608, 64, 608], P(None, 'blk', 'int'), may hold values from -6 to 6
- integrals: float32 [64, 608, 4, 608], P('int', None, None, 'blk'), may hold values from -0.078125 to 0.078125
- occ_irrep: int32 [64], replicated, may hold values from 0 to 7
- virt_irrep: int32 [608], replicated, may hold values from 0 to 7, as said below
- i_batch: int32 [4], replicated, may hold values from 0 to 63
- j_batch: int32 [4], replicated, may hold values from 0 to 63
Outputs:
- residual: float32 [4, 608, 4, 608], P(None, 'blk', None, 'int')
Inputs may be any that keep to these rules, and one draw needn't show every extreme that they name: `occ_irrep`: labels of the eight D2h irreps; the product of two irreps is the bitwise exclusive or of their labels. `virt_irrep`: labels of the eight D2h irreps, combined as above; no irrep labels more than 96 virtual orbitals, and one labels exactly 96. `i_batch`: positions among the 64 occupied orbitals. `j_batch`: positions among the 64 occupied orbitals.
All inputs are finite; a program needn't handle non-finite values.
Results may differ from a plain program's by a relative error of at most 0.00007.
Values sent between devices are 32-bit elements; how exact they have to be, the bound alone decides.
A program may use at most 128 MiB of HBM per device.

v0:
```python
import jax
import jax.numpy as jnp
from jax import lax
from jax.sharding import PartitionSpec as P


def lookup(labels, where_at):
    positions = jnp.arange(labels.shape[0], dtype=jnp.int32)
    onehot = (where_at[:, None] == positions[None, :]).astype(jnp.int32)
    return jnp.sum(onehot * labels[None, :], axis=1)


def per_device(amplitudes, integrals, occ_irrep, virt_irrep, i_batch, j_batch):
    a_count = amplitudes.shape[1]
    k_count = amplitudes.shape[2]
    a_start = lax.axis_index("blk") * a_count
    k_start = lax.axis_index("int") * k_count
    occ_k = lax.dynamic_slice_in_dim(occ_irrep, k_start, k_count)
    virt_a = lax.dynamic_slice_in_dim(virt_irrep, a_start, a_count)
    irr_i = lookup(occ_irrep, i_batch)
    irr_j = lookup(occ_irrep, j_batch)
    left_pair = jnp.bitwise_xor(irr_i[:, None, None, None], occ_k[None, None, :, None])
    amp_keep = left_pair == jnp.bitwise_xor(
        virt_a[None, :, None, None], virt_irrep[None, None, None, :]
    )
    swap_keep = left_pair == jnp.bitwise_xor(
        virt_irrep[None, :, None, None], virt_a[None, None, None, :]
    )
    sym_amp = jnp.where(amp_keep, amplitudes, 0.0)
    moved = lax.all_to_all(amplitudes, "blk", split_axis=3, concat_axis=1, tiled=True)
    sym_moved = jnp.where(swap_keep, moved, 0.0)
    occ_virt = jnp.bitwise_xor(occ_k[:, None, None, None], virt_irrep[None, :, None, None])
    int_keep = occ_virt == jnp.bitwise_xor(
        irr_j[None, None, :, None], virt_irrep[None, None, None, :]
    )
    sym_piece = jnp.where(int_keep, lax.all_gather(integrals, "blk", axis=3, tiled=True), 0.0)
    cycle = jnp.einsum("iakc,kcjb->iajb", sym_amp, sym_piece, precision=lax.Precision.HIGHEST)
    swapped = jnp.einsum("icka,kcjb->iajb", sym_moved, sym_piece, precision=lax.Precision.HIGHEST)
    terms = jnp.stack((cycle, swapped))
    summed = lax.psum_scatter(terms, "int", scatter_dimension=4, tiled=True)
    return 2.0 * summed[0] - summed[1]


def solution(mesh):
    placed = (P(None, "blk", "int", None), P("int", None, None, "blk"), P(), P(), P(), P())
    return jax.shard_map(
        per_device,
        mesh=mesh,
        in_specs=placed,
        out_specs=P(None, "blk", None, "int"),
        check_vma=False,
    )
```

profile of v0, /device:TPU:2, one launch (start us, length us, event | category | flops | bytes accessed | tf_op | source)
XLA Modules:
  0.0 368.6 jit_solution(17444483353083959431)
XLA Ops:
  6.5 0.0 all-gather.2.cloned.1.call-start
  6.5 0.7 all-gather.2.cloned.1.call-update
  7.3 4.9 %copy.50 = f32[4,19,4,608]{1,2,0,3:T(4,128)} copy(f32[4,19,4,608]{3,2,1,0:T(4,128)} %param.6) | data formatting | bytes 1478656 | tf_op args[0]
  12.1 7.6 %reshape.168 = f32[32,1,5776]{2,1,0:T(1,128)} reshape(f32[608,4,4,19]{3,2,1,0:T(4,128)} %bitcast.42) | data formatting | bytes 1478656
  19.8 9.5 %all-to-all-start = ((f32[32,1,5776]{2,1,0:T(1,128)}), f32[32,1,5776]{2,1,0:T(1,128)S(1)}, u32[]{:S(2)}, u32[]{:S(2)}) async-start(f32[32,1,5776]{2,1,0:T(1,128)} %reshape.168), calls=%async_computation | async-start | bytes 1507328 | tf_op jit(solution)/shard_map/all_to_all | solution.py:30
  29.2 0.0 all-reduce.3.cloned.1.call-start
  29.3 0.7 dynamic_slice.6
  30.0 0.9 select_reduce_fusion.1
  30.9 0.8 broadcast_xor_fusion.3
  31.7 0.2 copy.47
  31.9 0.8 dynamic_slice.7
  32.6 0.1 broadcast_xor_fusion.4
  32.7 0.8 broadcast_xor_fusion
  33.5 0.8 broadcast_xor_fusion.1
  34.2 1.4 select_bitcast_fusion.1
  35.7 10.2 %all-to-all-done = f32[32,1,5776]{2,1,0:T(1,128)S(1)} async-done(((f32[32,1,5776]{2,1,0:T(1,128)}), f32[32,1,5776]{2,1,0:T(1,128)S(1)}, u32[]{:S(2)}, u32[]{:S(2)}) %all-to-all-start) | async-done | bytes 739360 | tf_op jit(solution)/shard_map/all_to_all | solution.py:30
  45.9 0.5 broadcast.124
  46.4 2.4 reduce
  48.9 8.0 %reshape.169 = f32[608,4,4,19]{3,2,1,0:T(4,128)} reshape(f32[32,5776]{1,0:T(8,128)S(1)} %reduce) | data formatting | bytes 1478656
  56.9 6.2 %copy.73 = f32[4,19,4,32,19]{1,3,2,4,0:T(8,128)} copy(f32[4,19,4,32,19]{1,2,0,4,3:T(4,128)} %bitcast.40) | data formatting | bytes 1478656 | tf_op jit(solution)/shard_map/all_to_all | solution.py:30
  63.1 6.0 %all_to_all.16 = f32[4,608,4,19]{1,2,3,0:T(4,128)S(1)} reshape(f32[4,32,19,4,19]{2,1,3,4,0:T(8,128)} %bitcast.41) | data formatting | bytes 1478656 | tf_op jit(solution)/shard_map/all_to_all | solution.py:30
  69.1 0.3 select_bitcast_fusion
  69.4 57.0 %all-gather.2.cloned.1.call-done = f32[4,608,4,608]{1,2,3,0:T(4,128)} async-done(((f32[4,608,4,19]{1,2,3,0:T(4,128)}), f32[4,608,4,608]{1,2,3,0:T(4,128)}) %all-gather.2.cloned.1.call-update) | async-done | bytes 23658512 | tf_op jit(solution)/shard_map/all_gather | solution.py:36
  126.3 22.7 %compare_select_fusion = f32[4,608,4,608]{1,2,3,0:T(4,128)} fusion(f32[4,608,4,608]{1,2,3,0:T(4,128)} %all-gather.2.cloned.1.call-done, s32[4,608]{0,1:T(8,128)S(1)} %copy.47, s32[4,608]{1,0:T(4,128)S(1)} %get-tuple-element.7), kind=kLoop, calls=%fused_computation.4 | loop fusion | flops 11829248 | bytes 47336448 | tf_op jit(solution)/shard_map/jit(_where)/select_n | solution.py:36
  149.0 30.2 %copy.49 = f32[4,608,4,608]{3,1,0,2:T(8,128)} copy(f32[4,608,4,608]{1,2,3,0:T(4,128)} %compare_select_fusion) | data formatting | bytes 47316992 | tf_op jit(solution)/shard_map/jit(_where)/select_n | solution.py:36
  179.2 18.0 %fusion.7 = f32[1,4,19,4,608]{4,2,3,1,0:T(8,128)S(1)} fusion(f32[4,608,4,608]{3,1,0,2:T(8,128)} %copy.49, f32[4,608,4,19,1]{1,2,3,0,4:T(4,128)S(1)} %select_bitcast_fusion), kind=kOutput, calls=%fused_computation.8 | convolution fusion | flops 5394137088 | bytes 25137152 | tf_op jit(solution)/shard_map/icka,kcjb->iajb/dot_general | solution.py:38
  197.3 18.1 %fusion.4 = f32[1,4,19,4,608]{4,2,3,1,0:T(8,128)S(1)} fusion(f32[4,608,4,608]{3,1,0,2:T(8,128)} %copy.49, f32[4,19,4,608,1]{3,2,1,0,4:T(4,128)S(1)} %select_bitcast_fusion.1), kind=kOutput, calls=%fused_computation.7 | convolution fusion | flops 5394137088 | bytes 25137152 | tf_op jit(solution)/shard_map/iakc,kcjb->iajb/dot_general | solution.py:37
  215.4 1.4 pad_maximum_fusion
  216.8 0.0 all-reduce.3.cloned.1.call-update
  216.8 1.3 dynamic-slice
  218.7 141.1 %all-reduce.3.cloned.1.call-done = f32[2,4,19,4,608]{4,2,3,1,0:T(8,128)} async-done(((f32[2,4,19,4,608]{4,2,3,1,0:T(8,128)}), f32[2,4,19,4,608]{4,2,3,1,0:T(8,128)}) %all-reduce.3.cloned.1.call-update) | async-done | bytes 1478672
  359.8 1.3 fusion.12
  361.1 0.7 copy.55
Async XLA Ops:
  6.5 119.8 %all-gather.2.cloned.1.call-start = ((), (), s32[]{:S(2)}) async-start(), calls=%async_computation.1 | async-start | bytes 25681920 | tf_op jit(solution)/shard_map/all_gather | solution.py:36
  19.8 26.2 %all-to-all-start = ((f32[32,1,5776]{2,1,0:T(1,128)}), f32[32,1,5776]{2,1,0:T(1,128)S(1)}, u32[]{:S(2)}, u32[]{:S(2)}) async-start(f32[32,1,5776]{2,1,0:T(1,128)} %reshape.168), calls=%async_computation | async-start | bytes 1507328 | tf_op jit(solution)/shard_map/all_to_all | solution.py:30
  29.2 330.6 %all-reduce.3.cloned.1.call-start = ((), (), s32[]{:S(2)}) async-start(), calls=%async_computation.2 | async-start | bytes 3932160
Sparse Core Ops, SparseCore 0:
  10.6 115.7 all-gather.1
  216.9 142.8 all-reduce.2
where the time goes:
time: 370 us; the launch traced here: 369 us
  waiting for transfers between devices  209 us (56%)
  local copies, waits for them, and re-layouts  67.1 us (18%)
  matrix products  36.1 us (10%)
  other arithmetic  32.8 us (9%)
  between operations  14.1 us (4%)
  starting transfers between devices  9.52 us (3%)
    unnamed x3, waiting for transfers between devices  142 us
    all_gather x1, waiting for transfers between devices, per_device(): lax.all_gather(integrals, 'blk', axis=3, tiled=True)  57 us
    select_n x1, local copies, waits for them, and re-layouts, per_device(): jnp.where(int_keep, lax.all_gather(integrals, 'blk', axis=3, tiled=True),...  30.2 us
    select_n x1, other arithmetic, per_device(): jnp.where(int_keep, lax.all_gather(integrals, 'blk', axis=3, tiled=True),...  22.7 us
    unnamed x4, local copies, waits for them, and re-layouts  21.8 us
    dot_general x1, matrix products, per_device(): jnp.einsum('iakc,kcjb->iajb', sym_amp, sym_piece, precision=lax.Precision...  18.1 us
    dot_general x1, matrix products, per_device(): jnp.einsum('icka,kcjb->iajb', sym_moved, sym_piece, precision=lax.Precisi...  18 us
    all_to_all x3, local copies, waits for them, and re-layouts, per_device(): lax.all_to_all(amplitudes, 'blk', split_axis=3, concat_axis=1, tiled=True)  12.7 us
  transfers between devices with their start and end apart: 3, of which 3 were waited for; matrix products, arithmetic and copies ran while one was open for 10% of the time, Pallas kernels for 0%

commit v1 on v0

v1 whole, which is shorter than its diff:
```python
import jax
import jax.numpy as jnp
from jax import lax
from jax.experimental import pallas as pl
from jax.experimental.pallas import tpu as pltpu
from jax.sharding import PartitionSpec as P

MESH = pl.DeviceIdType.MESH
F32 = jnp.float32
BF16 = jnp.bfloat16
CAP = 96
NI = 4
NJ = 4
NA = 19
NK = 4
NB = 38
NV = 608
BLK = 32
INT = 16
ROWS = 80
CPAD = 24


def lookup(labels, where_at):
    positions = jnp.arange(labels.shape[0], dtype=jnp.int32)
    onehot = (where_at[:, None] == positions[None, :]).astype(jnp.int32)
    return jnp.sum(onehot * labels[None, :], axis=1)


def halves(x):
    high = x.astype(BF16)
    return high, (x - high.astype(F32)).astype(BF16)


def nn(a, b):
    return jnp.dot(a, b, preferred_element_type=F32)


def kernel(
    g_ref, at_ref, d_ref, pt_ref, irrc_ref, skia_ref, sbj_ref, sia_ref, code_ref, codez_ref, sjb_ref, siac_ref,
    out_ref,
    gbuf, dbuf, rbuf, ebuf, zsend, zrecv, ysum, ygath,
    g_send, g_recv, f_send, f_recv, d_send, d_recv, z_send, z_recv, y_send, y_recv,
):
    me = lax.axis_index("blk")
    mz = lax.axis_index("int")
    core = me % 2
    chip = me // 2
    cy = chip // 4
    cx = chip % 4
    sibling = me + 1 - 2 * core

    barrier = pltpu.get_barrier_semaphore()

    def greet_blk(n, c):
        pl.semaphore_signal(barrier, inc=1, device_id=((me + n) % BLK, mz), device_id_type=MESH)
        return c

    def greet_int(n, c):
        pl.semaphore_signal(barrier, inc=1, device_id=(me, (mz + n) % INT), device_id_type=MESH)
        return c

    lax.fori_loop(1, BLK, greet_blk, 0)
    lax.fori_loop(1, INT, greet_int, 0)
    pl.semaphore_wait(barrier, BLK - 1 + INT - 1)

    def at_offset(o, sign):
        return (((cy + sign * (o // 4) + 4) % 4) * 4 + (cx + sign * (o % 4) + 4) % 4) * 2 + core

    def g_copy(o):
        return pltpu.make_async_remote_copy(
            src_ref=g_ref, dst_ref=gbuf.at[me], send_sem=g_send.at[o], recv_sem=g_recv.at[o],
            device_id=(at_offset(o, 1), mz), device_id_type=MESH,
        )

    def f_copy(o):
        slot = at_offset(o, -1)
        return pltpu.make_async_remote_copy(
            src_ref=gbuf.at[slot], dst_ref=gbuf.at[slot], send_sem=f_send.at[o], recv_sem=f_recv.at[o],
            device_id=(sibling, mz), device_id_type=MESH,
        )

    own_forward = pltpu.make_async_remote_copy(
        src_ref=g_ref, dst_ref=gbuf.at[me], send_sem=f_send.at[0], recv_sem=f_recv.at[0],
        device_id=(sibling, mz), device_id_type=MESH,
    )

    def d_copy(n):
        target = (me + n) % BLK
        return pltpu.make_async_remote_copy(
            src_ref=d_ref.at[target], dst_ref=dbuf.at[me], send_sem=d_send.at[n], recv_sem=d_recv.at[n],
            device_id=(target, mz), device_id_type=MESH,
        )

    def z_copy(n):
        target = (mz + n) % INT
        return pltpu.make_async_remote_copy(
            src_ref=zsend.at[target], dst_ref=zrecv.at[mz], send_sem=z_send.at[n], recv_sem=z_recv.at[n],
            device_id=(me, target), device_id_type=MESH,
        )

    def y_copy(n):
        target = (mz + n) % INT
        return pltpu.make_async_remote_copy(
            src_ref=ysum, dst_ref=ygath.at[mz], send_sem=y_send.at[n], recv_sem=y_recv.at[n],
            device_id=(me, target), device_id_type=MESH,
        )

    def each(first, last, do):
        def body(n, c):
            do(n)
            return c

        lax.fori_loop(first, last, body, 0)

    each(1, 16, lambda o: g_copy(o).start())
    own_forward.start()
    each(1, BLK, lambda n: d_copy(n).start())

    gbuf[me] = g_ref[...]
    dbuf[me] = d_ref[me]

    @pl.loop(0, 10)
    def _(n):
        at = pl.ds(pl.multiple_of(n * 256, 256), 256)
        row = lax.broadcasted_iota(jnp.int32, (NJ * CAP, 256), 0)
        ebuf[:, at] = jnp.where(row == code_ref[:, at], 1.0, 0.0).astype(BF16)

    def pass_on(o):
        g_copy(o).wait_recv()
        f_copy(o).start()

    each(1, 16, pass_on)
    each(1, BLK, lambda n: d_copy(n).wait_recv())

    swapped = jnp.where(irrc_ref[...] == skia_ref[...], dbuf[...].reshape(BLK * CPAD, 384), 0.0)
    s_high, s_low = halves(swapped)
    s_t = nn(pt_ref[...], s_high) + nn(pt_ref[...], s_low)
    t_t = 2.0 * at_ref[...] - s_t
    w = jnp.concatenate([t_t[:, k * ROWS:(k + 1) * ROWS] for k in range(NK)], axis=0)
    w = jnp.concatenate([w, jnp.zeros((NK * CAP, 128 - ROWS), F32)], axis=1)
    w_high, w_low = halves(w)

    own_forward.wait_recv()
    each(1, 16, lambda o: f_copy(o).wait_recv())

    @pl.loop(0, 8)
    def _(n):
        g_high, g_low = halves(gbuf[pl.ds(n * 4, 4)].reshape(4 * ROWS, NK * CAP))
        r = nn(g_high, w_high) + (nn(g_high, w_low) + nn(g_low, w_high))
        at = pl.ds(pl.multiple_of(n * 4 * ROWS, 4 * ROWS), 4 * ROWS)
        rbuf[at] = jnp.where(sbj_ref[at] == sia_ref[...], r, 0.0)

    r_high, r_low = halves(rbuf[...])
    packed = nn(ebuf[...], r_high) + nn(ebuf[...], r_low)
    turned = packed.T[:ROWS]
    for block in range(3):
        for group in range(5):
            zsend[block * 5 + group] = turned[group * 16:(group + 1) * 16, block * 128:(block + 1) * 128]
    zsend[15] = jnp.zeros((16, 128), F32)

    each(1, INT, lambda n: z_copy(n).start())
    zrecv[mz] = zsend[mz]
    each(1, INT, lambda n: z_copy(n).wait_recv())
    total = zrecv[0]
    for n in range(1, INT):
        total = total + zrecv[n]
    ysum[...] = total
    each(1, INT, lambda n: y_copy(n).start())
    ygath[mz] = total
    row = lax.broadcasted_iota(jnp.int32, (NJ * CAP, 256), 0)
    spread = jnp.where(row == codez_ref[...], 1.0, 0.0).astype(BF16)
    each(1, INT, lambda n: y_copy(n).wait_recv())
    whole = jnp.concatenate(
        [jnp.concatenate([ygath[block * 5 + group] for group in range(5)], axis=0) for block in range(3)], axis=1
    )
    y_high, y_low = halves(whole)
    out = nn(y_high, spread) + nn(y_low, spread)
    out_ref[...] = jnp.where(siac_ref[...] == sjb_ref[...], out, 0.0)

    each(1, 16, lambda o: g_copy(o).wait_send())
    own_forward.wait_send()
    each(1, 16, lambda o: f_copy(o).wait_send())
    each(1, BLK, lambda n: d_copy(n).wait_send())
    each(1, INT, lambda n: z_copy(n).wait_send())
    each(1, INT, lambda n: y_copy(n).wait_send())


def pad_to(x, shape, value=0):
    return jnp.pad(x, [(0, n - m) for n, m in zip(shape, x.shape)], constant_values=value)


def per_device(amplitudes, integrals, occ_irrep, virt_irrep, i_batch, j_batch):
    blk = lax.axis_index("blk")
    z = lax.axis_index("int")
    occ_k = lax.dynamic_slice_in_dim(occ_irrep, z * NK, NK)
    virt_a = lax.dynamic_slice_in_dim(virt_irrep, blk * NA, NA)
    irr_i = lookup(occ_irrep, i_batch)
    irr_j = lookup(occ_irrep, j_batch)
    orbital = jnp.arange(NV, dtype=jnp.int32)
    alike = (virt_irrep[:, None] == virt_irrep[None, :]) & (orbital[None, :] < orbital[:, None])
    place = jnp.sum(alike.astype(jnp.int32), axis=1)
    onehot = (place[:, None] == jnp.arange(CAP, dtype=jnp.int32)[None, :]).astype(F32)

    s_ika = jnp.bitwise_xor(
        jnp.bitwise_xor(irr_i[:, None, None], occ_k[None, None, :]), virt_a[None, :, None]
    )
    sym_amp = jnp.where(s_ika[..., None] == virt_irrep, amplitudes, 0.0)
    amp_t = jnp.einsum("iakc,cp->pkia", sym_amp, onehot, precision=lax.Precision.HIGHEST)
    amp_t = pad_to(amp_t.reshape(CAP, NK, NI * NA), (CAP, NK, ROWS)).reshape(CAP, NK * ROWS)
    amp_t = pad_to(amp_t, (CAP, 384))

    g = jnp.transpose(integrals, (0, 3, 2, 1))
    s_kbj = jnp.bitwise_xor(
        jnp.bitwise_xor(occ_k[:, None, None], virt_a[None, :, None]), irr_j[None, None, :]
    )
    sym_g = jnp.where(s_kbj[..., None] == virt_irrep, g, 0.0)
    g_p = jnp.einsum("kbjc,cp->bjkp", sym_g, onehot, precision=lax.Precision.HIGHEST)
    g_p = pad_to(g_p.reshape(NA * NJ, NK * CAP), (ROWS, NK * CAP))

    moved = jnp.transpose(amplitudes.reshape(NI, NA, NK, BLK, NA), (3, 1, 2, 0, 4)).reshape(BLK, NA, NK, NI * NA)
    moved = pad_to(pad_to(moved, (BLK, CPAD, NK, ROWS)).reshape(BLK, CPAD, NK * ROWS), (BLK, CPAD, 384))

    p_t = pad_to(onehot.reshape(BLK, NA, CAP), (BLK, CPAD, CAP)).reshape(BLK * CPAD, CAP).T.astype(BF16)
    irr_c = pad_to(virt_irrep.reshape(BLK, NA), (BLK, CPAD), -1).reshape(BLK * CPAD, 1)
    s_kia = jnp.transpose(s_ika, (2, 0, 1)).reshape(NK, NI * NA)
    s_kia = pad_to(pad_to(s_kia, (NK, ROWS), -2).reshape(1, NK * ROWS), (1, 384), -2)

    s_bj = jnp.bitwise_xor(virt_irrep[:, None], irr_j[None, :]).reshape(BLK, NA * NJ)
    s_bj = pad_to(s_bj, (BLK, ROWS), -1).reshape(BLK * ROWS, 1)
    s_ia = jnp.bitwise_xor(irr_i[:, None], virt_a[None, :]).reshape(1, NI * NA)
    code = (place[:, None] + CAP * jnp.arange(NJ, dtype=jnp.int32)[None, :]).reshape(BLK, NA * NJ)
    code = pad_to(code, (BLK, ROWS), -1).reshape(1, BLK * ROWS)

    virt_b = lax.dynamic_slice_in_dim(virt_irrep, z * NB, NB)
    place_b = lax.dynamic_slice_in_dim(place, z * NB, NB)
    codez = (place_b[None, :] + CAP * jnp.arange(NJ, dtype=jnp.int32)[:, None]).reshape(1, NJ * NB)
    s_jb = jnp.bitwise_xor(irr_j[:, None], virt_b[None, :]).reshape(1, NJ * NB)

    vmem = pl.BlockSpec(memory_space=pltpu.VMEM)
    dma = pltpu.SemaphoreType.DMA
    out = pl.pallas_call(
        kernel,
        out_shape=jax.ShapeDtypeStruct((ROWS, 256), F32),
        in_specs=[vmem] * 12,
        out_specs=vmem,
        scratch_shapes=[
            pltpu.VMEM((BLK, ROWS, NK * CAP), F32),
            pltpu.VMEM((BLK, CPAD, 384), F32),
            pltpu.VMEM((BLK * ROWS, 128), F32),
            pltpu.VMEM((NJ * CAP, BLK * ROWS), BF16),
            pltpu.VMEM((INT, 16, 128), F32),
            pltpu.VMEM((INT, 16, 128), F32),
            pltpu.VMEM((16, 128), F32),
            pltpu.VMEM((INT, 16, 128), F32),
            dma((16,)), dma((16,)), dma((16,)), dma((16,)), dma((BLK,)), dma((BLK,)),
            dma((INT,)), dma((INT,)), dma((INT,)), dma((INT,)),
        ],
        compiler_params=pltpu.CompilerParams(
            collective_id=0, has_side_effects=True, vmem_limit_bytes=48 * 1024 * 1024
        ),
    )(
        g_p, amp_t, moved, p_t, irr_c, s_kia, s_bj, pad_to(s_ia, (1, 128), -2), code,
        pad_to(codez, (1, 256), -1), pad_to(s_jb, (1, 256), -1), pad_to(s_ia, (1, ROWS), -2).reshape(ROWS, 1),
    )
    return out[:NI * NA, :NJ * NB].reshape(NI, NA, NJ, NB)


def solution(mesh):
    placed = (P(None, "blk", "int", None), P("int", None, None, "blk"), P(), P(), P(), P())
    return jax.shard_map(
        per_device,
        mesh=mesh,
        in_specs=placed,
        out_specs=P(None, "blk", None, "int"),
        check_vma=False,
    )
```

time: 370 us -> 116 us (0.31)
  the two profiles are of different devices: /device:TPU:2 before, /device:TPU:1 now
where the time goes in v1:
time: 116 us
  Pallas kernels  87.8 us (76%)
  local copies, waits for them, and re-layouts  22.8 us (20%)
  other arithmetic  3.76 us (3%)
  matrix products  1.23 us (1%)
    pallas_call x1, Pallas kernels, per_device(): pl.pallas_call(kernel, out_shape=jax.ShapeDtypeStruct((ROWS, 256), F32),...  87.8 us
    reshape x1, local copies, waits for them, and re-layouts, per_device(): amplitudes.reshape(NI, NA, NK, BLK, NA)  7.35 us
    transpose x1, local copies, waits for them, and re-layouts, per_device(): jnp.transpose(amplitudes.reshape(NI, NA, NK, BLK, NA), (3, 1, 2, 0, 4))  4.3 us
    unnamed x8, local copies, waits for them, and re-layouts  3.44 us

profile of v1, /device:TPU:1, one launch (start us, length us, event | category | flops | bytes accessed | tf_op | source)
XLA Modules:
  0.0 116.0 jit_solution(16049283630817544154)
XLA Ops:
  0.0 0.8 dynamic_slice.13
  0.8 0.7 dynamic_slice.12
  1.5 0.9 select_reduce_fusion
  2.4 0.1 broadcast_xor_fusion.6
  2.5 0.1 broadcast_xor_fusion.4
  2.5 0.1 broadcast_xor_fusion
  2.6 0.0 copy-start.1
  2.6 1.8 %compare_select_fusion = (f32[4,19,4,608]{3,2,1,0:T(4,128)S(1)}, f32[4,19,4,608]{3,2,1,0:T(4,128)S(1)}) fusion(f32[4,19,4,608]{3,2,1,0:T(4,128)} %param.6, s32[4,19,4]{2,1,0:T(8,128)S(1)} %get-tuple-element.13, s32[608]{0:T(1024)} %param.9, f32[4,608,4,19]{1,2,3,0:T(4,128)} %param.7, s32[4,19,4]{2,1,0:T(8,128)S(1)} %get-tuple-element.14), kind=kLoop, calls=%fused_computation.8 | loop fusion | flops 739328 | bytes 2962176 | tf_op jit(solution)/shard_map/jit(_where)/select_n | solution.py:208
  4.5 0.0 copy-done.1
  4.5 0.3 convert_reduce_fusion
  4.8 0.6 convolution_bitcast_fusion.1
  5.4 0.1 copy.29
  5.5 0.1 reshape.216
  5.6 0.0 copy-start
  5.7 0.6 convolution_bitcast_fusion
  6.4 0.1 copy.33
  6.5 0.2 copy-done
  6.8 7.4 %reshape.219 = f32[4,19,4,32,19]{4,3,2,1,0:T(8,128)} reshape(f32[4,19,4,608]{3,2,1,0:T(4,128)S(1)} %copy-done) | data formatting | bytes 1478656 | tf_op jit(solution)/shard_map/reshape | solution.py:221
  14.1 4.3 %copy.34 = f32[32,19,4,4,19]{0,2,4,3,1:T(4,128)S(1)} copy(f32[32,19,4,4,19]{4,0,2,1,3:T(8,128)} %bitcast.27) | data formatting | bytes 1478656 | tf_op jit(solution)/shard_map/transpose | solution.py:221
  18.4 3.0 %copy.46 = f32[32,19,4,76]{3,2,1,0:T(4,128)} copy(f32[32,19,4,76]{0,2,3,1:T(4,128)S(1)} %bitcast.28) | data formatting | bytes 1478656
  21.4 1.7 %pad.64.clone = f32[32,24,4,80]{3,2,1,0:T(4,128)S(1)} pad(f32[32,19,4,76]{3,2,1,0:T(4,128)} %copy.46, f32[]{:T(128)} %constant.29.clone.1), padding=0_0x0_5x0_0x0_4 | pad | bytes 1722372 | tf_op jit(solution)/shard_map/jit(_pad)/pad | solution.py:190
  23.1 0.7 reshape.221
  23.9 0.1 pad.65.d_ref
  24.0 0.1 eq.102
  24.1 0.2 iota_compare_fusion.1
  24.3 0.1 convert_convert_fusion
  24.3 0.1 copy.36
  24.5 0.1 reshape.222
  24.6 0.2 reshape.230.irrc_ref
  24.8 0.1 xor.168
  24.8 0.1 xor.169
  24.9 0.1 xor.170
  25.0 0.1 reshape.224
  25.1 0.1 copy.37
  25.2 0.1 xor.176
  25.3 0.1 broadcast_xor_fusion.2
  25.4 0.1 copy.47
  25.5 0.6 reshape.231.sbj_ref
  26.1 0.1 xor.181
  26.2 0.1 copy.39
  26.3 0.1 add.86
  26.4 0.1 broadcast_add_fusion
  26.5 0.1 copy.48
  26.6 0.1 reshape.226.code_ref
  26.7 0.1 dynamic_slice.14
  26.8 0.1 broadcast_add_fusion.1
  26.9 0.1 add.93
  26.9 0.1 dynamic_slice.15
  27.0 0.1 broadcast_xor_fusion.3
  27.1 0.1 xor.185
  27.2 0.1 copy.43.siac_ref
  27.3 87.8 %shard_map.64 = f32[80,256]{1,0:T(8,128)S(1)} custom-call(f32[80,384]{1,0:T(8,128)S(1)} %pad.61.g_ref, f32[96,384]{1,0:T(8,128)S(1)} %pad.63.at_ref, f32[32,24,384]{2,1,0:T(8,128)S(1)} %pad.65.d_ref, bf16[96,768]{1,0:T(8,128)(2,1)S(1)} %bitcast.25, s32[768,1]{1,0:T(8,128)S(1)} %reshape.230.irrc_ref, s32[1,384]{1,0:T(1,128)S(1)} %pad.70.skia_ref, ...), custom_call_target="tpu_custom_call" | custom-call | tf_op jit(solution)/shard_map/pallas_call | solution.py:242
  115.2 0.8 reshape.228
  (23 shorter events, 0.2 us)
Async XLA Ops:
  2.6 1.8 %copy-start.1 = (s32[608]{0:T(1024)S(1)}, s32[608]{0:T(1024)}, u32[]{:S(2)}) copy-start(s32[608]{0:T(1024)} %param.9) | copy-start | bytes 7300
  5.6 1.1 copy-start

commit v2 on v1

v2 whole, which is shorter than its diff:
```python
import jax
import jax.numpy as jnp
from jax import lax
from jax.experimental import pallas as pl
from jax.experimental.pallas import tpu as pltpu
from jax.sharding import PartitionSpec as P

MESH = pl.DeviceIdType.MESH
F32 = jnp.float32
BF16 = jnp.bfloat16
CAP = 96
NI = 4
NJ = 4
NA = 19
NK = 4
NB = 38
NV = 608
BLK = 32
INT = 16
ROWS = 80
CPAD = 24
HALF = 40
GROUP = 320
PITCH = 21


def lookup(labels, where_at):
    positions = jnp.arange(labels.shape[0], dtype=jnp.int32)
    onehot = (where_at[:, None] == positions[None, :]).astype(jnp.int32)
    return jnp.sum(onehot * labels[None, :], axis=1)


def halves(x):
    high = x.astype(BF16)
    return high, (x - high.astype(F32)).astype(BF16)


def nn(a, b):
    return jnp.dot(a, b, preferred_element_type=F32)


def kernel(
    g_ref, at_ref, a_ref, pt_ref, irrc_ref, skia_ref, sbj_ref, sia_ref, code_ref, codez_ref, sjb_ref, siac_ref,
    out_ref,
    gh0, gh1, spaced, moved, dbuf, ebuf, acc, zsend, zrecv, ysum, ygath,
    own_sem, p0_send, p0_recv, p1_send, p1_recv, q0_send, q0_recv, q1_send, q1_recv,
    s0_send, s0_recv, s1_send, s1_recv, d_send, d_recv, z_send, z_recv, y_send, y_recv,
):
    me = lax.axis_index("blk")
    mz = lax.axis_index("int")
    core = me % 2
    cx = (me // 2) % 4
    cy = me // 8

    def plane(y, x, c):
        return ((((y + 4) % 4) * 4 + (x + 4) % 4) * 2 + c, mz)

    def each(first, last, do):
        def body(n, c):
            do(n)
            return c

        lax.fori_loop(first, last, body, 0)

    def remote(src, dst, send, recv, device):
        return pltpu.make_async_remote_copy(
            src_ref=src, dst_ref=dst, send_sem=send, recv_sem=recv, device_id=device, device_id_type=MESH
        )

    barrier = pltpu.get_barrier_semaphore()

    def greet(device):
        pl.semaphore_signal(barrier, inc=1, device_id=device, device_id_type=MESH)

    each(1, INT, lambda n: greet((me, (mz + n) % INT)))
    each(1, BLK, lambda n: greet(((me + n) % BLK, mz)))

    own0 = pltpu.make_async_copy(g_ref.at[pl.ds(0, HALF)], gh0.at[cy, core, cx], own_sem.at[0])
    own1 = pltpu.make_async_copy(g_ref.at[pl.ds(HALF, HALF)], gh1.at[cx, core, cy], own_sem.at[1])
    own0.start()
    own1.start()

    lane = lax.broadcasted_iota(jnp.int32, (NV, 1024), 1)
    source = jnp.where(lane % 32 < NA, NA * (lane // 32) + lane % 32, -1)
    respace = jnp.where(lax.broadcasted_iota(jnp.int32, (NV, 1024), 0) == source, 1.0, 0.0).astype(BF16)
    a_high, a_low = halves(a_ref[...])
    spaced[...] = nn(a_high, respace) + nn(a_low, respace)

    pl.semaphore_wait(barrier, BLK - 1 + INT - 1)

    def p0(o):
        return remote(g_ref.at[pl.ds(0, HALF)], gh0.at[cy, core, cx], p0_send.at[o], p0_recv.at[o], plane(cy, cx + o, core))

    def p1(o):
        return remote(g_ref.at[pl.ds(HALF, HALF)], gh1.at[cx, core, cy], p1_send.at[o], p1_recv.at[o], plane(cy + o, cx, core))

    each(1, 4, lambda o: p0(o).start())
    each(1, 4, lambda o: p1(o).start())

    def d_copy(d):
        return remote(moved.at[d], dbuf.at[me], d_send.at[d], d_recv.at[me], (d, mz))

    def d_start(d):
        @pl.when(d != me)
        def _():
            d_copy(d).start()

    def d_tile(step):
        return (me // 4 + step) % 8

    small = lax.broadcasted_iota(jnp.int32, (CPAD, 128), 1)

    def shuffle(step, c):
        tile = d_tile(step)
        at = pl.ds(pl.multiple_of(tile * 128, 128), 128)
        blocks = [spaced[m * CPAD:(m + 1) * CPAD, at] for m in range(NI * NK)]
        for part in range(4):
            for t in range(3):
                held = jnp.zeros((CPAD, 128), F32)
                here = blocks[6 * t:6 * t + 6]
                for n, block in enumerate(here):
                    shift = (PITCH * n - 32 * part) % 128
                    turned = pltpu.roll(block, shift, 1) if shift else block
                    held = jnp.where((small >= PITCH * n) & (small < PITCH * n + NA), turned, held)
                moved[4 * tile + part, :, t * 128:(t + 1) * 128] = held

        @pl.when(step > 0)
        def _():
            each(0, 4, lambda n: d_start(4 * d_tile(step + 7) + n))

        return c

    lax.fori_loop(0, 8, shuffle, 0)
    each(0, 4, lambda n: d_start(4 * d_tile(7) + n))
    dbuf[me] = moved[me]

    def q0(o):
        dev = plane(cy + 1 - 2 * o, cx, core)
        return remote(gh0.at[cy, core], gh0.at[cy, core], q0_send.at[o], q0_recv.at[o], dev)

    def q1(o):
        dev = plane(cy, cx + 1 - 2 * o, core)
        return remote(gh1.at[cx, core], gh1.at[cx, core], q1_send.at[o], q1_recv.at[o], dev)

    def r0(o):
        row = (cy + 3 + 2 * o) % 4
        part = pl.ds(2 * o, 2)
        ref = gh0.at[row, core, part]
        return remote(ref, ref, q0_send.at[2 + o], q0_recv.at[2 + o], plane(cy + 1 - 2 * o, cx, core))

    def r1(o):
        row = (cx + 3 + 2 * o) % 4
        part = pl.ds(2 * o, 2)
        ref = gh1.at[row, core, part]
        return remote(ref, ref, q1_send.at[2 + o], q1_recv.at[2 + o], plane(cy, cx + 1 - 2 * o, core))

    sibling = plane(cy, cx, 1 - core)
    order = (0, 3, 1, 2)

    def s0(n):
        ref = gh0.at[(cy + order[n]) % 4, core]
        return remote(ref, ref, s0_send.at[n], s0_recv.at[n], sibling)

    def s1(n):
        ref = gh1.at[(cx + order[n]) % 4, core]
        return remote(ref, ref, s1_send.at[n], s1_recv.at[n], sibling)

    own0.wait()
    each(1, 4, lambda o: p0(o).wait_recv())
    q0(0).start()
    q0(1).start()
    s0(0).start()
    own1.wait()
    each(1, 4, lambda o: p1(o).wait_recv())
    q1(0).start()
    q1(1).start()
    s1(0).start()

    @pl.loop(0, 8)
    def _(n):
        row = lax.broadcasted_iota(jnp.int32, (NJ * CAP, GROUP), 0)
        ebuf[n] = jnp.where(row == code_ref[n], 1.0, 0.0).astype(BF16)

    def d_wait(n):
        d = (me + n) % BLK
        remote(moved.at[d], dbuf.at[d], d_send.at[d], d_recv.at[d], (d, mz)).wait_recv()

    each(1, BLK, d_wait)
    swapped = jnp.where(irrc_ref[...] == skia_ref[...], dbuf[...].reshape(BLK * CPAD, 384), 0.0)
    s_high, s_low = halves(swapped)
    s_t = nn(pt_ref[...], s_high) + nn(pt_ref[...], s_low)
    t_t = 2.0 * at_ref[...] - s_t
    columns = []
    for k in range(NK):
        first = [128 * ((NI * k + i) // 6) + PITCH * ((NI * k + i) % 6) for i in range(NI)]
        columns.append(jnp.concatenate([t_t[:, f:f + NA] for f in first], axis=1))
    w = jnp.concatenate(columns, axis=0)
    w = jnp.concatenate([w, jnp.zeros((NK * CAP, 128 - NI * NA), F32)], axis=1)
    w_high, w_low = halves(w)

    acc[...] = jnp.zeros_like(acc)

    def product(piece, n):
        g_high, g_low = halves(piece.reshape(GROUP, NK * CAP))
        r = nn(g_high, w_high) + (nn(g_high, w_low) + nn(g_low, w_high))
        r_high, r_low = halves(jnp.where(sbj_ref[n] == sia_ref[...], r, 0.0))
        acc[...] += nn(ebuf[n], r_high) + nn(ebuf[n], r_low)

    def product0(n):
        s0(n).wait_recv()
        row = (cy + order[n]) % 4
        product(gh0[row], row)

    def product1(n):
        s1(n).wait_recv()
        row = (cx + order[n]) % 4
        product(gh1[row], 4 + row)

    q0(0).wait_recv()
    r0(0).start()
    s0(1).start()
    q1(0).wait_recv()
    r1(0).start()
    s1(1).start()
    q0(1).wait_recv()
    r0(1).start()
    s0(2).start()
    q1(1).wait_recv()
    r1(1).start()
    s1(2).start()
    for n in range(3):
        product0(n)
        product1(n)
    r0(0).wait_recv()
    r0(1).wait_recv()
    s0(3).start()
    r1(0).wait_recv()
    r1(1).wait_recv()
    s1(3).start()
    product0(3)
    product1(3)

    def z_copy(n):
        target = (mz + n) % INT
        return remote(zsend.at[target], zrecv.at[mz], z_send.at[n], z_recv.at[n], (me, target))

    def y_copy(n):
        target = (mz + n) % INT
        return remote(ysum, ygath.at[mz], y_send.at[n], y_recv.at[n], (me, target))

    turned = acc[...].T[:ROWS]
    for block in range(3):
        for group in range(5):
            zsend[block * 5 + group] = turned[group * 16:(group + 1) * 16, block * 128:(block + 1) * 128]
    zsend[15] = jnp.zeros((16, 128), F32)

    each(1, INT, lambda n: z_copy((n + 7) % 15 + 1).start())
    zrecv[mz] = zsend[mz]
    each(1, INT, lambda n: z_copy(n).wait_recv())
    total = zrecv[0]
    for n in range(1, INT):
        total = total + zrecv[n]
    ysum[...] = total
    each(1, INT, lambda n: y_copy((n + 7) % 15 + 1).start())
    ygath[mz] = total
    row = lax.broadcasted_iota(jnp.int32, (NJ * CAP, 256), 0)
    spread = jnp.where(row == codez_ref[...], 1.0, 0.0).astype(BF16)
    each(1, INT, lambda n: y_copy(n).wait_recv())
    whole = jnp.concatenate(
        [jnp.concatenate([ygath[block * 5 + group] for group in range(5)], axis=0) for block in range(3)], axis=1
    )
    y_high, y_low = halves(whole)
    out = nn(y_high, spread) + nn(y_low, spread)
    out_ref[...] = jnp.where(siac_ref[...] == sjb_ref[...], out, 0.0)

    each(1, 4, lambda o: p0(o).wait_send())
    each(1, 4, lambda o: p1(o).wait_send())
    for o in range(2):
        q0(o).wait_send()
        q1(o).wait_send()
        r0(o).wait_send()
        r1(o).wait_send()
    for n in range(4):
        s0(n).wait_send()
        s1(n).wait_send()
    each(1, BLK, lambda n: d_copy((me + n) % BLK).wait_send())
    each(1, INT, lambda n: z_copy(n).wait_send())
    each(1, INT, lambda n: y_copy(n).wait_send())


def pad_to(x, shape, value=0):
    return jnp.pad(x, [(0, n - m) for n, m in zip(shape, x.shape)], constant_values=value)


def blocks_of_six(x, value):
    x = pad_to(x, (x.shape[0], 18, PITCH), value).reshape(-1, 3, 6 * PITCH)
    return pad_to(x, (x.shape[0], 3, 128), value).reshape(-1, 384)


def by_group(x):
    x = x.reshape(4, 4, 2, 2, HALF)
    first = jnp.transpose(x[:, :, :, 0], (0, 2, 1, 3)).reshape(4, GROUP)
    second = jnp.transpose(x[:, :, :, 1], (1, 2, 0, 3)).reshape(4, GROUP)
    return jnp.concatenate([first, second], axis=0)


def per_device(amplitudes, integrals, occ_irrep, virt_irrep, i_batch, j_batch):
    blk = lax.axis_index("blk")
    z = lax.axis_index("int")
    occ_k = lax.dynamic_slice_in_dim(occ_irrep, z * NK, NK)
    virt_a = lax.dynamic_slice_in_dim(virt_irrep, blk * NA, NA)
    irr_i = lookup(occ_irrep, i_batch)
    irr_j = lookup(occ_irrep, j_batch)
    orbital = jnp.arange(NV, dtype=jnp.int32)
    alike = (virt_irrep[:, None] == virt_irrep[None, :]) & (orbital[None, :] < orbital[:, None])
    place = jnp.sum(alike.astype(jnp.int32), axis=1)
    onehot = (place[:, None] == jnp.arange(CAP, dtype=jnp.int32)[None, :]).astype(F32)

    s_ika = jnp.bitwise_xor(
        jnp.bitwise_xor(irr_i[:, None, None], occ_k[None, None, :]), virt_a[None, :, None]
    )
    sym_amp = jnp.where(s_ika[..., None] == virt_irrep, amplitudes, 0.0)
    amp_t = jnp.einsum("iakc,cp->pkia", sym_amp, onehot, precision=lax.Precision.HIGHEST)
    amp_t = blocks_of_six(amp_t.reshape(CAP, NK * NI, NA), 0)

    g = jnp.transpose(integrals, (0, 3, 2, 1))
    s_kbj = jnp.bitwise_xor(
        jnp.bitwise_xor(occ_k[:, None, None], virt_a[None, :, None]), irr_j[None, None, :]
    )
    sym_g = jnp.where(s_kbj[..., None] == virt_irrep, g, 0.0)
    g_p = jnp.einsum("kbjc,cp->bjkp", sym_g, onehot, precision=lax.Precision.HIGHEST)
    g_p = pad_to(g_p.reshape(NA * NJ, NK * CAP), (ROWS, NK * CAP))

    a_rows = pad_to(jnp.transpose(amplitudes, (2, 0, 1, 3)), (NK, NI, CPAD, NV)).reshape(NK * NI * CPAD, NV)

    p_t = pad_to(onehot.reshape(BLK, NA, CAP), (BLK, CPAD, CAP)).reshape(BLK * CPAD, CAP).T.astype(BF16)
    irr_c = pad_to(virt_irrep.reshape(BLK, NA), (BLK, CPAD), -1).reshape(BLK * CPAD, 1)
    s_kia = blocks_of_six(jnp.transpose(s_ika, (2, 0, 1)).reshape(1, NK * NI, NA), -2)

    s_bj = jnp.bitwise_xor(virt_irrep[:, None], irr_j[None, :]).reshape(BLK, NA * NJ)
    s_bj = by_group(pad_to(s_bj, (BLK, ROWS), -1)).reshape(8, GROUP, 1)
    s_ia = jnp.bitwise_xor(irr_i[:, None], virt_a[None, :]).reshape(1, NI * NA)
    code = (place[:, None] + CAP * jnp.arange(NJ, dtype=jnp.int32)[None, :]).reshape(BLK, NA * NJ)
    code = by_group(pad_to(code, (BLK, ROWS), -1)).reshape(8, 1, GROUP)

    virt_b = lax.dynamic_slice_in_dim(virt_irrep, z * NB, NB)
    place_b = lax.dynamic_slice_in_dim(place, z * NB, NB)
    codez = (place_b[None, :] + CAP * jnp.arange(NJ, dtype=jnp.int32)[:, None]).reshape(1, NJ * NB)
    s_jb = jnp.bitwise_xor(irr_j[:, None], virt_b[None, :]).reshape(1, NJ * NB)

    vmem = pl.BlockSpec(memory_space=pltpu.VMEM)
    dma = pltpu.SemaphoreType.DMA
    out = pl.pallas_call(
        kernel,
        out_shape=jax.ShapeDtypeStruct((ROWS, 256), F32),
        in_specs=[vmem] * 12,
        out_specs=vmem,
        scratch_shapes=[
            pltpu.VMEM((4, 2, 4, HALF, NK * CAP), F32),
            pltpu.VMEM((4, 2, 4, HALF, NK * CAP), F32),
            pltpu.VMEM((NI * NK * CPAD, 1024), F32),
            pltpu.VMEM((BLK, CPAD, 384), F32),
            pltpu.VMEM((BLK, CPAD, 384), F32),
            pltpu.VMEM((8, NJ * CAP, GROUP), BF16),
            pltpu.VMEM((NJ * CAP, 128), F32),
            pltpu.VMEM((INT, 16, 128), F32),
            pltpu.VMEM((INT, 16, 128), F32),
            pltpu.VMEM((16, 128), F32),
            pltpu.VMEM((INT, 16, 128), F32),
            dma((2,)), dma((4,)), dma((4,)), dma((4,)), dma((4,)), dma((4,)), dma((4,)), dma((4,)), dma((4,)),
            dma((4,)), dma((4,)), dma((4,)), dma((4,)), dma((BLK,)), dma((BLK,)),
            dma((INT,)), dma((INT,)), dma((INT,)), dma((INT,)),
        ],
        compiler_params=pltpu.CompilerParams(
            collective_id=0, has_side_effects=True, vmem_limit_bytes=48 * 1024 * 1024
        ),
    )(
        g_p, amp_t, a_rows, p_t, irr_c, s_kia, s_bj, pad_to(s_ia, (1, 128), -2), code,
        pad_to(codez, (1, 256), -1), pad_to(s_jb, (1, 256), -1), pad_to(s_ia, (1, ROWS), -2).reshape(ROWS, 1),
    )
    return out[:NI * NA, :NJ * NB].reshape(NI, NA, NJ, NB)


def solution(mesh):
    placed = (P(None, "blk", "int", None), P("int", None, None, "blk"), P(), P(), P(), P())
    return jax.shard_map(
        per_device,
        mesh=mesh,
        in_specs=placed,
        out_specs=P(None, "blk", None, "int"),
        check_vma=False,
    )
```

time: 116 us -> 84.7 us (0.73)
  local copies, waits for them, and re-layouts: 22.8 us -> 6.6 us
  Pallas kernels: 87.8 us -> 72.4 us
    pallas_call x1, Pallas kernels: 87.8 us -> 72.4 us  [per_device(): pl.pallas_call(kernel, out_shape=jax.ShapeDtypeStruct((ROWS, 256), F32),...]
    reshape x6 -> x11, local copies, waits for them, and re-layouts: 9.01 us -> 1.2 us  [the longest x1 0.43 us: per_device(): s_bj = by_group(pad_to(s_bj, (BLK, ROWS), -1)).reshape(8, GROUP, 1)]
    transpose x1 -> x4, local copies, waits for them, and re-layouts: 4.3 us -> 0.02 us  [the longest x2 0.01 us: by_group(): second = jnp.transpose(x[:, :, :, 1], (1, 2, 0, 3)).reshape(4, GROUP)]
    unnamed x8 -> x10, local copies, waits for them, and re-layouts: 3.44 us -> 1.06 us
    pad x13 -> x11, local copies, waits for them, and re-layouts: 1.87 us -> 0.17 us  [pad_to(): jnp.pad(x, [(0, n - m) for n, m in zip(shape, x.shape)], constant_values=...]
where the time goes in v2:
time: 84.7 us; the launch traced here: 84.5 us
  Pallas kernels  72.4 us (85%)
  local copies, waits for them, and re-layouts  6.6 us (8%)
  other arithmetic  3.85 us (5%)
  matrix products  1.23 us (1%)
    pallas_call x1, Pallas kernels, per_device(): pl.pallas_call(kernel, out_shape=jax.ShapeDtypeStruct((ROWS, 256), F32),...  72.4 us
    select_n x1, other arithmetic, per_device(): sym_amp = jnp.where(s_ika[..., None] == virt_irrep, amplitudes, 0.0)  1.81 us

profile of v2, /device:TPU:1, one launch (start us, length us, event | category | flops | bytes accessed | tf_op | source)
XLA Modules:
  0.0 84.5 jit_solution(9125360943376933752)
XLA Ops:
  0.0 0.8 dynamic_slice.13
  0.8 0.7 dynamic_slice.12
  1.5 0.9 %select_reduce_fusion = (s32[4]{0:T(128)S(1)}, s32[4]{0:T(128)S(1)}) fusion(s32[4]{0:T(128)} %param.10, s32[64]{0:T(128)} %param.8, s32[4]{0:T(128)} %param.11), kind=kLoop, calls=%fused_computation.23 | loop fusion | flops 1528 | bytes 320 | tf_op jit(solution)/shard_map/reduce_sum | solution.py:30
  2.4 0.1 broadcast_xor_fusion.6
  2.5 0.1 broadcast_xor_fusion.5
  2.5 0.1 broadcast_xor_fusion
  2.6 0.0 copy-start.1
  2.6 1.8 %compare_select_fusion = (f32[4,19,4,608]{3,2,1,0:T(4,128)S(1)}, f32[4,19,4,608]{3,2,1,0:T(4,128)S(1)}) fusion(f32[4,19,4,608]{3,2,1,0:T(4,128)} %param.6, s32[4,19,4]{2,1,0:T(8,128)S(1)} %get-tuple-element.17, s32[608]{0:T(1024)} %param.9, f32[4,608,4,19]{1,2,3,0:T(4,128)} %param.7, s32[4,19,4]{2,1,0:T(8,128)S(1)} %get-tuple-element.18), kind=kLoop, calls=%fused_computation.8 | loop fusion | flops 739328 | bytes 2962176 | tf_op jit(solution)/shard_map/jit(_where)/select_n | solution.py:322
  4.5 0.0 copy-done.1
  4.5 0.3 convert_reduce_fusion
  4.8 0.6 convolution_bitcast_fusion.1
  5.4 0.1 copy.51
  5.5 0.1 reshape.269
  5.6 0.6 convolution_bitcast_fusion
  6.3 0.0 copy-start
  6.3 0.1 copy.53
  6.4 0.1 copy.71
  6.5 0.1 copy.70.at_ref
  6.7 0.8 copy-done
  7.4 0.1 copy.72
  7.5 0.1 pad.60.clone
  7.6 0.1 eq.102
  7.7 0.2 iota_compare_fusion.1
  7.8 0.1 convert_convert_fusion
  7.9 0.1 copy.57
  8.1 0.1 reshape.274
  8.2 0.2 reshape.289.irrc_ref
  8.3 0.1 xor.174
  8.4 0.1 broadcast_xor_fusion.3
  8.5 0.1 reshape.276
  8.6 0.1 copy.58
  8.7 0.1 xor.181
  8.8 0.1 broadcast_xor_fusion.2
  8.9 0.1 copy.73
  9.0 0.1 reshape.278
  9.1 0.1 reshape.280
  9.2 0.1 reshape.279
  9.3 0.4 copy.67.sbj_ref
  9.8 0.1 xor.186
  9.9 0.1 copy.62
  10.0 0.1 add.84
  10.1 0.1 broadcast_add_fusion
  10.2 0.1 copy.74
  10.3 0.1 reshape.282
  10.4 0.1 reshape.284
  10.5 0.1 reshape.283
  10.6 0.1 dynamic_slice.14
  10.7 0.1 broadcast_add_fusion.1
  10.8 0.1 add.91
  10.9 0.1 dynamic_slice.15
  11.0 0.1 broadcast_xor_fusion.4
  11.0 0.1 xor.190
  11.1 0.1 copy.68.siac_ref
  11.2 72.4 %shard_map.64 = f32[80,256]{1,0:T(8,128)S(1)} custom-call(f32[80,384]{1,0:T(8,128)S(1)} %pad.57.g_ref, f32[96,384]{1,0:T(8,128)S(1)} %copy.70.at_ref, f32[384,608]{1,0:T(8,128)S(1)} %bitcast.46, bf16[96,768]{1,0:T(8,128)(2,1)S(1)} %bitcast.47, s32[768,1]{1,0:T(8,128)S(1)} %reshape.289.irrc_ref, s32[1,384]{1,0:T(1,128)S(1)} %bitcast.49, ...), custom_call_target="tpu_custom_call" | custom-call | tf_op jit(solution)/shard_map/pallas_call | solution.py:353
  83.7 0.8 reshape.287
  (30 shorter events, 0.3 us)
Async XLA Ops:
  2.6 1.8 %copy-start.1 = (s32[608]{0:T(1024)S(1)}, s32[608]{0:T(1024)}, u32[]{:S(2)}) copy-start(s32[608]{0:T(1024)} %param.9) | copy-start | bytes 7300
  6.3 1.1 %copy-start = (f32[4,19,4,608]{3,2,1,0:T(4,128)S(1)}, f32[4,19,4,608]{3,2,1,0:T(4,128)}, u32[]{:S(2)}) copy-start(f32[4,19,4,608]{3,2,1,0:T(4,128)} %param.6) | copy-start | bytes 2217988

commit v3 on v2

--- a/solution.py
+++ b/solution.py
@@ -21,6 +21,7 @@
 CPAD = 24
 HALF = 40
 GROUP = 320
+FAR_FIRST = (8, 7, 9, 6, 10, 5, 11, 4, 12, 3, 13, 2, 14, 1, 15)
 PITCH = 21
 
 
@@ -39,10 +40,15 @@
     return jnp.dot(a, b, preferred_element_type=F32)
 
 
+def nt(a, b):
+    return lax.dot_general(a, b, (((1,), (1,)), ((), ())), preferred_element_type=F32)
+
+
 def kernel(
-    g_ref, at_ref, a_ref, pt_ref, irrc_ref, skia_ref, sbj_ref, sia_ref, code_ref, codez_ref, sjb_ref, siac_ref,
+    int_ref, skbj_ref, a_ref, skiac_ref, virt_ref, place_ref, placed_ref, irrc_ref, skia_ref, row_ref, column_ref, sia_ref,
+    rowz_ref, siac_ref,
     out_ref,
-    gh0, gh1, spaced, moved, dbuf, ebuf, acc, zsend, zrecv, ysum, ygath,
+    g_ref, g_rows, gh0, gh1, spaced, moved, dbuf, arrived, ebuf, acc, zsend, zrecv, ysum, ygath,
     own_sem, p0_send, p0_recv, p1_send, p1_recv, q0_send, q0_recv, q1_send, q1_recv,
     s0_send, s0_recv, s1_send, s1_recv, d_send, d_recv, z_send, z_recv, y_send, y_recv,
 ):
@@ -77,16 +83,36 @@
 
     own0 = pltpu.make_async_copy(g_ref.at[pl.ds(0, HALF)], gh0.at[cy, core, cx], own_sem.at[0])
     own1 = pltpu.make_async_copy(g_ref.at[pl.ds(HALF, HALF)], gh1.at[cx, core, cy], own_sem.at[1])
+
+    def onehot(places):
+        row = lax.broadcasted_iota(jnp.int32, (CAP, places.shape[1]), 0)
+        return jnp.where(row == places, 1.0, 0.0).astype(BF16)
+
+    p_all = onehot(place_ref[...])
+    for k in range(NK):
+        for b in range(NA):
+            g_rows[k, b * NJ:(b + 1) * NJ] = int_ref[k, b]
+        g_rows[k, NA * NJ:] = jnp.zeros((ROWS - NA * NJ, NV), F32)
+    packed = []
+    for k in range(NK):
+        high, low = halves(jnp.where(skbj_ref[k] == virt_ref[...], g_rows[k], 0.0))
+        packed.append(nt(high, p_all) + nt(low, p_all))
+    g_ref[...] = jnp.concatenate(packed, axis=1)
+    high, low = halves(jnp.where(skiac_ref[...] == virt_ref[...], a_ref[...], 0.0))
+    direct = nt(p_all, high) + nt(p_all, low)
+    p_t = onehot(placed_ref[...])
+
+    a_high, a_low = halves(a_ref[...])
+    for n in range(4):
+        lane = lax.broadcasted_iota(jnp.int32, (1, 256), 1)
+        source = jnp.where(lane % 32 < NA, NA * (8 * n + lane // 32) + lane % 32, -1)
+        respace = jnp.where(lax.broadcasted_iota(jnp.int32, (NV, 256), 0) == source, 1.0, 0.0).astype(BF16)
+        spaced[:, n * 256:(n + 1) * 256] = nn(a_high, respace) + nn(a_low, respace)
+
+    pl.semaphore_wait(barrier, BLK - 1 + INT - 1)
+
     own0.start()
     own1.start()
-
-    lane = lax.broadcasted_iota(jnp.int32, (NV, 1024), 1)
-    source = jnp.where(lane % 32 < NA, NA * (lane // 32) + lane % 32, -1)
-    respace = jnp.where(lax.broadcasted_iota(jnp.int32, (NV, 1024), 0) == source, 1.0, 0.0).astype(BF16)
-    a_high, a_low = halves(a_ref[...])
-    spaced[...] = nn(a_high, respace) + nn(a_low, respace)
-
-    pl.semaphore_wait(barrier, BLK - 1 + INT - 1)
 
     def p0(o):
         return remote(g_ref.at[pl.ds(0, HALF)], gh0.at[cy, core, cx], p0_send.at[o], p0_recv.at[o], plane(cy, cx + o, core))
@@ -122,7 +148,7 @@
                     shift = (PITCH * n - 32 * part) % 128
                     turned = pltpu.roll(block, shift, 1) if shift else block
                     held = jnp.where((small >= PITCH * n) & (small < PITCH * n + NA), turned, held)
-                moved[4 * tile + part, :, t * 128:(t + 1) * 128] = held
+                moved[4 * tile + part, :, t * 128:(t + 1) * 128] = held[:NA]
 
         @pl.when(step > 0)
         def _():
@@ -155,14 +181,16 @@
         return remote(ref, ref, q1_send.at[2 + o], q1_recv.at[2 + o], plane(cy, cx + 1 - 2 * o, core))
 
     sibling = plane(cy, cx, 1 - core)
-    order = (0, 3, 1, 2)
+
+    def order(n):
+        return n + n // 2 - 2 * (n // 3)
 
     def s0(n):
-        ref = gh0.at[(cy + order[n]) % 4, core]
+        ref = gh0.at[(cy + order(n)) % 4, core]
         return remote(ref, ref, s0_send.at[n], s0_recv.at[n], sibling)
 
     def s1(n):
-        ref = gh1.at[(cx + order[n]) % 4, core]
+        ref = gh1.at[(cx + order(n)) % 4, core]
         return remote(ref, ref, s1_send.at[n], s1_recv.at[n], sibling)
 
     own0.wait()
@@ -179,21 +207,25 @@
     @pl.loop(0, 8)
     def _(n):
         row = lax.broadcasted_iota(jnp.int32, (NJ * CAP, GROUP), 0)
-        ebuf[n] = jnp.where(row == code_ref[n], 1.0, 0.0).astype(BF16)
+        ebuf[n] = jnp.where(row == row_ref[n] // 8, 1.0, 0.0).astype(BF16)
 
     def d_wait(n):
         d = (me + n) % BLK
         remote(moved.at[d], dbuf.at[d], d_send.at[d], d_recv.at[d], (d, mz)).wait_recv()
 
     each(1, BLK, d_wait)
-    swapped = jnp.where(irrc_ref[...] == skia_ref[...], dbuf[...].reshape(BLK * CPAD, 384), 0.0)
+    for d in range(BLK):
+        arrived[d * CPAD:d * CPAD + NA] = dbuf[d]
+    swapped = jnp.where(irrc_ref[...] == skia_ref[...], arrived[...], 0.0)
     s_high, s_low = halves(swapped)
-    s_t = nn(pt_ref[...], s_high) + nn(pt_ref[...], s_low)
-    t_t = 2.0 * at_ref[...] - s_t
+    s_t = nn(p_t, s_high) + nn(p_t, s_low)
     columns = []
     for k in range(NK):
-        first = [128 * ((NI * k + i) // 6) + PITCH * ((NI * k + i) % 6) for i in range(NI)]
-        columns.append(jnp.concatenate([t_t[:, f:f + NA] for f in first], axis=1))
+        pairs = []
+        for m in range(NI * k, NI * k + NI):
+            first = 128 * (m // 6) + PITCH * (m % 6)
+            pairs.append(2.0 * direct[:, m * CPAD:m * CPAD + NA] - s_t[:, first:first + NA])
+        columns.append(jnp.concatenate(pairs, axis=1))
     w = jnp.concatenate(columns, axis=0)
     w = jnp.concatenate([w, jnp.zeros((NK * CAP, 128 - NI * NA), F32)], axis=1)
     w_high, w_low = halves(w)
@@ -203,42 +235,47 @@
     def product(piece, n):
         g_high, g_low = halves(piece.reshape(GROUP, NK * CAP))
         r = nn(g_high, w_high) + (nn(g_high, w_low) + nn(g_low, w_high))
-        r_high, r_low = halves(jnp.where(sbj_ref[n] == sia_ref[...], r, 0.0))
+        r_high, r_low = halves(jnp.where(column_ref[n] % 8 == sia_ref[...], r, 0.0))
         acc[...] += nn(ebuf[n], r_high) + nn(ebuf[n], r_low)
 
     def product0(n):
         s0(n).wait_recv()
-        row = (cy + order[n]) % 4
+        row = (cy + order(n)) % 4
         product(gh0[row], row)
 
     def product1(n):
         s1(n).wait_recv()
-        row = (cx + order[n]) % 4
+        row = (cx + order(n)) % 4
         product(gh1[row], 4 + row)
 
+    q0(1).wait_recv()
+    r0(1).start()
+    s0(1).start()
+    q1(1).wait_recv()
+    r1(1).start()
+    s1(1).start()
     q0(0).wait_recv()
     r0(0).start()
-    s0(1).start()
+    s0(2).start()
     q1(0).wait_recv()
     r1(0).start()
-    s1(1).start()
-    q0(1).wait_recv()
-    r0(1).start()
-    s0(2).start()
-    q1(1).wait_recv()
-    r1(1).start()
     s1(2).start()
-    for n in range(3):
+
+    def products(n, c):
+        @pl.when(n == 3)
+        def _():
+            r0(0).wait_recv()
+            r0(1).wait_recv()
+            s0(3).start()
+            r1(0).wait_recv()
+            r1(1).wait_recv()
+            s1(3).start()
+
         product0(n)
         product1(n)
-    r0(0).wait_recv()
-    r0(1).wait_recv()
-    s0(3).start()
-    r1(0).wait_recv()
-    r1(1).wait_recv()
-    s1(3).start()
-    product0(3)
-    product1(3)
+        return c
+
+    lax.fori_loop(0, 4, products, 0)
 
     def z_copy(n):
         target = (mz + n) % INT
@@ -254,24 +291,26 @@
             zsend[block * 5 + group] = turned[group * 16:(group + 1) * 16, block * 128:(block + 1) * 128]
     zsend[15] = jnp.zeros((16, 128), F32)
 
-    each(1, INT, lambda n: z_copy((n + 7) % 15 + 1).start())
+    for n in FAR_FIRST:
+        z_copy(n).start()
     zrecv[mz] = zsend[mz]
     each(1, INT, lambda n: z_copy(n).wait_recv())
     total = zrecv[0]
     for n in range(1, INT):
         total = total + zrecv[n]
     ysum[...] = total
-    each(1, INT, lambda n: y_copy((n + 7) % 15 + 1).start())
+    for n in FAR_FIRST:
+        y_copy(n).start()
     ygath[mz] = total
     row = lax.broadcasted_iota(jnp.int32, (NJ * CAP, 256), 0)
-    spread = jnp.where(row == codez_ref[...], 1.0, 0.0).astype(BF16)
+    spread = jnp.where(row == rowz_ref[...] // 8, 1.0, 0.0).astype(BF16)
     each(1, INT, lambda n: y_copy(n).wait_recv())
     whole = jnp.concatenate(
         [jnp.concatenate([ygath[block * 5 + group] for group in range(5)], axis=0) for block in range(3)], axis=1
     )
     y_high, y_low = halves(whole)
     out = nn(y_high, spread) + nn(y_low, spread)
-    out_ref[...] = jnp.where(siac_ref[...] == sjb_ref[...], out, 0.0)
+    out_ref[...] = jnp.where(siac_ref[...] == rowz_ref[...] % 8, out, 0.0)
 
     each(1, 4, lambda o: p0(o).wait_send())
     each(1, 4, lambda o: p1(o).wait_send())
@@ -314,53 +353,48 @@
     orbital = jnp.arange(NV, dtype=jnp.int32)
     alike = (virt_irrep[:, None] == virt_irrep[None, :]) & (orbital[None, :] < orbital[:, None])
     place = jnp.sum(alike.astype(jnp.int32), axis=1)
-    onehot = (place[:, None] == jnp.arange(CAP, dtype=jnp.int32)[None, :]).astype(F32)
-
     s_ika = jnp.bitwise_xor(
         jnp.bitwise_xor(irr_i[:, None, None], occ_k[None, None, :]), virt_a[None, :, None]
     )
-    sym_amp = jnp.where(s_ika[..., None] == virt_irrep, amplitudes, 0.0)
-    amp_t = jnp.einsum("iakc,cp->pkia", sym_amp, onehot, precision=lax.Precision.HIGHEST)
-    amp_t = blocks_of_six(amp_t.reshape(CAP, NK * NI, NA), 0)
-
-    g = jnp.transpose(integrals, (0, 3, 2, 1))
+    a_rows = pad_to(jnp.transpose(amplitudes, (2, 0, 1, 3)), (NK, NI, CPAD, NV)).reshape(NK * NI * CPAD, NV)
+    s_kia = jnp.transpose(s_ika, (2, 0, 1)).reshape(1, NK * NI, NA)
+    s_kia_column = pad_to(s_kia, (1, NK * NI, CPAD), -2).reshape(NK * NI * CPAD, 1)
+    s_kia = blocks_of_six(s_kia, -2)
+
+    ints = jnp.transpose(integrals, (0, 3, 2, 1))
     s_kbj = jnp.bitwise_xor(
         jnp.bitwise_xor(occ_k[:, None, None], virt_a[None, :, None]), irr_j[None, None, :]
     )
-    sym_g = jnp.where(s_kbj[..., None] == virt_irrep, g, 0.0)
-    g_p = jnp.einsum("kbjc,cp->bjkp", sym_g, onehot, precision=lax.Precision.HIGHEST)
-    g_p = pad_to(g_p.reshape(NA * NJ, NK * CAP), (ROWS, NK * CAP))
-
-    a_rows = pad_to(jnp.transpose(amplitudes, (2, 0, 1, 3)), (NK, NI, CPAD, NV)).reshape(NK * NI * CPAD, NV)
-
-    p_t = pad_to(onehot.reshape(BLK, NA, CAP), (BLK, CPAD, CAP)).reshape(BLK * CPAD, CAP).T.astype(BF16)
+    s_kbj = pad_to(s_kbj.reshape(NK, NA * NJ), (NK, ROWS), -2).reshape(NK, ROWS, 1)
+
+    placed = pad_to(place.reshape(BLK, NA), (BLK, CPAD), -1).reshape(1, BLK * CPAD)
     irr_c = pad_to(virt_irrep.reshape(BLK, NA), (BLK, CPAD), -1).reshape(BLK * CPAD, 1)
-    s_kia = blocks_of_six(jnp.transpose(s_ika, (2, 0, 1)).reshape(1, NK * NI, NA), -2)
-
-    s_bj = jnp.bitwise_xor(virt_irrep[:, None], irr_j[None, :]).reshape(BLK, NA * NJ)
-    s_bj = by_group(pad_to(s_bj, (BLK, ROWS), -1)).reshape(8, GROUP, 1)
     s_ia = jnp.bitwise_xor(irr_i[:, None], virt_a[None, :]).reshape(1, NI * NA)
-    code = (place[:, None] + CAP * jnp.arange(NJ, dtype=jnp.int32)[None, :]).reshape(BLK, NA * NJ)
-    code = by_group(pad_to(code, (BLK, ROWS), -1)).reshape(8, 1, GROUP)
-
+
+    offset = 8 * CAP * jnp.arange(NJ, dtype=jnp.int32)
+    pairs = 8 * place[:, None] + offset[None, :] + jnp.bitwise_xor(virt_irrep[:, None], irr_j[None, :])
+    pairs = by_group(pad_to(pairs.reshape(BLK, NA * NJ), (BLK, ROWS), -1))
     virt_b = lax.dynamic_slice_in_dim(virt_irrep, z * NB, NB)
     place_b = lax.dynamic_slice_in_dim(place, z * NB, NB)
-    codez = (place_b[None, :] + CAP * jnp.arange(NJ, dtype=jnp.int32)[:, None]).reshape(1, NJ * NB)
-    s_jb = jnp.bitwise_xor(irr_j[:, None], virt_b[None, :]).reshape(1, NJ * NB)
+    row_z = 8 * place_b[None, :] + offset[:, None] + jnp.bitwise_xor(irr_j[:, None], virt_b[None, :])
+    row_z = pad_to(row_z.reshape(1, NJ * NB), (1, 256), -1)
 
     vmem = pl.BlockSpec(memory_space=pltpu.VMEM)
     dma = pltpu.SemaphoreType.DMA
     out = pl.pallas_call(
         kernel,
         out_shape=jax.ShapeDtypeStruct((ROWS, 256), F32),
-        in_specs=[vmem] * 12,
+        in_specs=[vmem] * 14,
         out_specs=vmem,
         scratch_shapes=[
+            pltpu.VMEM((ROWS, NK * CAP), F32),
+            pltpu.VMEM((NK, ROWS, NV), F32),
             pltpu.VMEM((4, 2, 4, HALF, NK * CAP), F32),
             pltpu.VMEM((4, 2, 4, HALF, NK * CAP), F32),
             pltpu.VMEM((NI * NK * CPAD, 1024), F32),
-            pltpu.VMEM((BLK, CPAD, 384), F32),
-            pltpu.VMEM((BLK, CPAD, 384), F32),
+            pltpu.VMEM((BLK, NA, 384), F32),
+            pltpu.VMEM((BLK, NA, 384), F32),
+            pltpu.VMEM((BLK * CPAD, 384), F32),
             pltpu.VMEM((8, NJ * CAP, GROUP), BF16),
             pltpu.VMEM((NJ * CAP, 128), F32),
             pltpu.VMEM((INT, 16, 128), F32),
@@ -375,8 +409,9 @@
             collective_id=0, has_side_effects=True, vmem_limit_bytes=48 * 1024 * 1024
         ),
     )(
-        g_p, amp_t, a_rows, p_t, irr_c, s_kia, s_bj, pad_to(s_ia, (1, 128), -2), code,
-        pad_to(codez, (1, 256), -1), pad_to(s_jb, (1, 256), -1), pad_to(s_ia, (1, ROWS), -2).reshape(ROWS, 1),
+        ints, s_kbj, a_rows, s_kia_column, virt_irrep.reshape(1, NV), place.reshape(1, NV), placed, irr_c, s_kia,
+        pairs.reshape(8, 1, GROUP), pairs.reshape(8, GROUP, 1), pad_to(s_ia, (1, 128), -2), row_z,
+        pad_to(s_ia, (1, ROWS), -2).reshape(ROWS, 1),
     )
     return out[:NI * NA, :NJ * NB].reshape(NI, NA, NJ, NB)
 

time: 84.7 us -> 79.4 us (0.937)
  Pallas kernels: 72.4 us -> 68 us
  local copies, waits for them, and re-layouts: 6.6 us -> 8.35 us
  other arithmetic: 3.85 us -> 2.42 us
  matrix products: 1.23 us -> 0 us
    pallas_call x1, Pallas kernels: 72.4 us -> 68 us  [per_device(): pl.pallas_call(kernel, out_shape=jax.ShapeDtypeStruct((ROWS, 256), F32),...]
    select_n x1 -> x0, other arithmetic: 1.81 us -> none  [per_device(): sym_amp = jnp.where(s_ika[..., None] == virt_irrep, amplitudes, 0.0)]
    dot_general x2 -> x0, matrix products: 1.23 us -> none  [the longest x1 0.62 us: per_device(): jnp.einsum('kbjc,cp->bjkp', sym_g, onehot, precision=lax.Precision.HIGHEST)]
    reshape x4 -> x9, local copies, waits for them, and re-layouts: 0.69 us -> 1.58 us  [the longest x1 0.7 us: per_device(): virt_irrep.reshape(1, NV)]
where the time goes in v3:
time: 79.4 us; the launch traced here: 79 us
  Pallas kernels  68 us (86%)
  local copies, waits for them, and re-layouts  8.35 us (11%)
  other arithmetic  2.42 us (3%)
    pallas_call x1, Pallas kernels, per_device(): pl.pallas_call(kernel, out_shape=jax.ShapeDtypeStruct((ROWS, 256), F32),...  68 us

profile of v3, /device:TPU:1, one launch (start us, length us, event | category | flops | bytes accessed | tf_op | source)
XLA Modules:
  0.0 79.0 jit_solution(5166848563608659628)
XLA Ops:
  0.0 0.0 copy-start.1
  0.0 0.8 %dynamic_slice.13 = s32[19]{0:T(128)S(1)} dynamic-slice(s32[608]{0:T(1024)} %param.9, s32[]{:T(128)S(6)} %select_n.11), dynamic_slice_sizes={19} | dynamic-slice | bytes 156 | tf_op jit(solution)/shard_map/dynamic_slice | solution.py:350
  0.8 0.7 dynamic_slice.12
  1.6 0.8 dynamic_slice.15
  2.3 0.9 %select_reduce_fusion = (s32[4]{0:T(128)S(1)}, s32[4]{0:T(128)S(1)}) fusion(s32[4]{0:T(128)} %param.10, s32[64]{0:T(128)} %param.8, s32[4]{0:T(128)} %param.11), kind=kLoop, calls=%fused_computation.9 | loop fusion | flops 1528 | bytes 320 | tf_op jit(solution)/shard_map/reduce_sum | solution.py:31
  3.2 0.1 broadcast_xor_fusion.2
  3.3 0.1 xor.152
  3.4 0.7 reshape.265.virt_ref
  4.1 0.1 broadcast_xor_fusion.1
  4.2 0.1 xor.162
  4.3 1.0 %convert_reduce_fusion = s32[608]{0:T(1024)S(1)} fusion(s32[608]{0:T(1024)} %param.9), kind=kLoop, calls=%fused_computation | loop fusion | flops 1847712 | bytes 4864 | tf_op jit(solution)/shard_map/reduce_sum | solution.py:355
  5.3 0.1 dynamic-slice_multiply_fusion
  5.4 0.1 xor_add_fusion.1
  5.5 0.1 add.104
  5.6 0.1 broadcast_xor_fusion
  5.6 0.1 reshape.271
  5.8 0.1 add.95
  5.9 0.1 xor.146
  5.9 0.1 reshape.267
  6.0 0.8 reshape.269
  6.8 0.1 copy.24
  6.9 0.1 copy.23
  7.0 0.1 reshape.268.placed_ref
  7.2 0.1 xor_add_fusion
  7.3 0.1 copy.34
  7.4 0.1 reshape.273
  7.5 0.1 reshape.274
  7.6 0.1 reshape.275
  7.7 0.1 copy.32.siac_ref
  7.8 0.1 xor.143
  7.9 0.1 xor.144
  8.0 0.1 copy.28.skbj_ref
  8.2 0.1 reshape.280.skiac_ref
  8.3 0.2 reshape.281.irrc_ref
  8.5 0.0 copy-done.1
  8.5 0.1 copy.33
  8.6 0.1 pad.44.clone
  8.6 0.4 copy.31.column_ref
  9.1 0.0 copy-start
  9.1 1.1 %copy-done = f32[4,608,4,19]{1,2,3,0:T(4,128)S(1)} copy-done((f32[4,608,4,19]{1,2,3,0:T(4,128)S(1)}, f32[4,608,4,19]{1,2,3,0:T(4,128)}, u32[]{:S(2)}) %copy-start) | copy-done | bytes 739352
  10.2 68.0 %shard_map.64 = f32[80,256]{1,0:T(8,128)S(1)} custom-call(f32[4,19,4,608]{3,2,1,0:T(4,128)S(1)} %bitcast.26, s32[4,80,1]{2,1,0:T(8,128)S(1)} %copy.28.skbj_ref, f32[384,608]{1,0:T(8,128)S(1)} %bitcast.25, s32[384,1]{1,0:T(8,128)S(1)} %reshape.280.skiac_ref, s32[1,608]{1,0:T(1,128)S(1)} %reshape.265.virt_ref, s32[1,608]{1,0:T(1,128)S(1)} %reshape.266.place_ref, ...), custom_call_target="tpu_custom_call" | custom-call | tf_op jit(solution)/shard_map/pallas_call | solution.py:384
  78.2 0.8 %reshape.279 = f32[4,19,4,38]{3,2,1,0:T(4,128)} reshape(f32[76,152]{1,0:T(8,128)S(1)} %bitcast.27) | data formatting | bytes 92416 | tf_op jit(solution)/shard_map/reshape | solution.py:416
  (26 shorter events, 0.2 us)
Async XLA Ops:
  0.0 8.5 %copy-start.1 = (f32[4,19,4,608]{3,2,1,0:T(4,128)S(1)}, f32[4,19,4,608]{3,2,1,0:T(4,128)}, u32[]{:S(2)}) copy-start(f32[4,19,4,608]{3,2,1,0:T(4,128)} %param.6) | copy-start | bytes 2217988
  9.1 1.1 %copy-start = (f32[4,608,4,19]{1,2,3,0:T(4,128)S(1)}, f32[4,608,4,19]{1,2,3,0:T(4,128)}, u32[]{:S(2)}) copy-start(f32[4,608,4,19]{1,2,3,0:T(4,128)} %param.7) | copy-start | bytes 2217988

commit v4 on v3

--- a/solution.py
+++ b/solution.py
@@ -98,9 +98,19 @@
         high, low = halves(jnp.where(skbj_ref[k] == virt_ref[...], g_rows[k], 0.0))
         packed.append(nt(high, p_all) + nt(low, p_all))
     g_ref[...] = jnp.concatenate(packed, axis=1)
-    high, low = halves(jnp.where(skiac_ref[...] == virt_ref[...], a_ref[...], 0.0))
-    direct = nt(p_all, high) + nt(p_all, low)
-    p_t = onehot(placed_ref[...])
+    pl.semaphore_wait(barrier, BLK - 1 + INT - 1)
+
+    own0.start()
+    own1.start()
+
+    def p0(o):
+        return remote(g_ref.at[pl.ds(0, HALF)], gh0.at[cy, core, cx], p0_send.at[o], p0_recv.at[o], plane(cy, cx + o, core))
+
+    def p1(o):
+        return remote(g_ref.at[pl.ds(HALF, HALF)], gh1.at[cx, core, cy], p1_send.at[o], p1_recv.at[o], plane(cy + o, cx, core))
+
+    each(1, 4, lambda o: p0(o).start())
+    each(1, 4, lambda o: p1(o).start())
 
     a_high, a_low = halves(a_ref[...])
     for n in range(4):
@@ -108,20 +118,6 @@
         source = jnp.where(lane % 32 < NA, NA * (8 * n + lane // 32) + lane % 32, -1)
         respace = jnp.where(lax.broadcasted_iota(jnp.int32, (NV, 256), 0) == source, 1.0, 0.0).astype(BF16)
         spaced[:, n * 256:(n + 1) * 256] = nn(a_high, respace) + nn(a_low, respace)
-
-    pl.semaphore_wait(barrier, BLK - 1 + INT - 1)
-
-    own0.start()
-    own1.start()
-
-    def p0(o):
-        return remote(g_ref.at[pl.ds(0, HALF)], gh0.at[cy, core, cx], p0_send.at[o], p0_recv.at[o], plane(cy, cx + o, core))
-
-    def p1(o):
-        return remote(g_ref.at[pl.ds(HALF, HALF)], gh1.at[cx, core, cy], p1_send.at[o], p1_recv.at[o], plane(cy + o, cx, core))
-
-    each(1, 4, lambda o: p0(o).start())
-    each(1, 4, lambda o: p1(o).start())
 
     def d_copy(d):
         return remote(moved.at[d], dbuf.at[me], d_send.at[d], d_recv.at[me], (d, mz))
@@ -160,25 +156,25 @@
     each(0, 4, lambda n: d_start(4 * d_tile(7) + n))
     dbuf[me] = moved[me]
 
-    def q0(o):
-        dev = plane(cy + 1 - 2 * o, cx, core)
-        return remote(gh0.at[cy, core], gh0.at[cy, core], q0_send.at[o], q0_recv.at[o], dev)
-
-    def q1(o):
-        dev = plane(cy, cx + 1 - 2 * o, core)
-        return remote(gh1.at[cx, core], gh1.at[cx, core], q1_send.at[o], q1_recv.at[o], dev)
+    def q0(o, late):
+        ref = gh0.at[cy, core, pl.ds(2 * abs(o - late), 2)]
+        return remote(ref, ref, q0_send.at[2 * late + o], q0_recv.at[2 * late + o], plane(cy + 1 - 2 * o, cx, core))
+
+    def q1(o, late):
+        ref = gh1.at[cx, core, pl.ds(2 * abs(o - late), 2)]
+        return remote(ref, ref, q1_send.at[2 * late + o], q1_recv.at[2 * late + o], plane(cy, cx + 1 - 2 * o, core))
 
     def r0(o):
         row = (cy + 3 + 2 * o) % 4
         part = pl.ds(2 * o, 2)
         ref = gh0.at[row, core, part]
-        return remote(ref, ref, q0_send.at[2 + o], q0_recv.at[2 + o], plane(cy + 1 - 2 * o, cx, core))
+        return remote(ref, ref, q0_send.at[4 + o], q0_recv.at[4 + o], plane(cy + 1 - 2 * o, cx, core))
 
     def r1(o):
         row = (cx + 3 + 2 * o) % 4
         part = pl.ds(2 * o, 2)
         ref = gh1.at[row, core, part]
-        return remote(ref, ref, q1_send.at[2 + o], q1_recv.at[2 + o], plane(cy, cx + 1 - 2 * o, core))
+        return remote(ref, ref, q1_send.at[4 + o], q1_recv.at[4 + o], plane(cy, cx + 1 - 2 * o, core))
 
     sibling = plane(cy, cx, 1 - core)
 
@@ -195,19 +191,27 @@
 
     own0.wait()
     each(1, 4, lambda o: p0(o).wait_recv())
-    q0(0).start()
-    q0(1).start()
+    q0(0, 0).start()
+    q0(1, 0).start()
+    q0(0, 1).start()
+    q0(1, 1).start()
     s0(0).start()
     own1.wait()
     each(1, 4, lambda o: p1(o).wait_recv())
-    q1(0).start()
-    q1(1).start()
+    q1(0, 0).start()
+    q1(1, 0).start()
+    q1(0, 1).start()
+    q1(1, 1).start()
     s1(0).start()
 
     @pl.loop(0, 8)
     def _(n):
         row = lax.broadcasted_iota(jnp.int32, (NJ * CAP, GROUP), 0)
         ebuf[n] = jnp.where(row == row_ref[n] // 8, 1.0, 0.0).astype(BF16)
+
+    high, low = halves(jnp.where(skiac_ref[...] == virt_ref[...], a_ref[...], 0.0))
+    direct = nt(p_all, high) + nt(p_all, low)
+    p_t = onehot(placed_ref[...])
 
     def d_wait(n):
         d = (me + n) % BLK
@@ -248,18 +252,16 @@
         row = (cx + order(n)) % 4
         product(gh1[row], 4 + row)
 
-    q0(1).wait_recv()
-    r0(1).start()
-    s0(1).start()
-    q1(1).wait_recv()
-    r1(1).start()
-    s1(1).start()
-    q0(0).wait_recv()
-    r0(0).start()
-    s0(2).start()
-    q1(0).wait_recv()
-    r1(0).start()
-    s1(2).start()
+    for o in (1, 0):
+        q0(o, 0).wait_recv()
+        r0(o).start()
+        q1(o, 0).wait_recv()
+        r1(o).start()
+    for o in (1, 0):
+        q0(o, 1).wait_recv()
+        s0(2 - o).start()
+        q1(o, 1).wait_recv()
+        s1(2 - o).start()
 
     def products(n, c):
         @pl.when(n == 3)
@@ -315,8 +317,10 @@
     each(1, 4, lambda o: p0(o).wait_send())
     each(1, 4, lambda o: p1(o).wait_send())
     for o in range(2):
-        q0(o).wait_send()
-        q1(o).wait_send()
+        q0(o, 0).wait_send()
+        q0(o, 1).wait_send()
+        q1(o, 0).wait_send()
+        q1(o, 1).wait_send()
         r0(o).wait_send()
         r1(o).wait_send()
     for n in range(4):
@@ -346,7 +350,8 @@
 def per_device(amplitudes, integrals, occ_irrep, virt_irrep, i_batch, j_batch):
     blk = lax.axis_index("blk")
     z = lax.axis_index("int")
-    occ_k = lax.dynamic_slice_in_dim(occ_irrep, z * NK, NK)
+    occ_k = lookup(occ_irrep, z * NK + jnp.arange(NK, dtype=jnp.int32))
+    virt_irrep = lax.optimization_barrier(jnp.bitwise_and(virt_irrep, 7))
     virt_a = lax.dynamic_slice_in_dim(virt_irrep, blk * NA, NA)
     irr_i = lookup(occ_irrep, i_batch)
     irr_j = lookup(occ_irrep, j_batch)
@@ -401,7 +406,7 @@
             pltpu.VMEM((INT, 16, 128), F32),
             pltpu.VMEM((16, 128), F32),
             pltpu.VMEM((INT, 16, 128), F32),
-            dma((2,)), dma((4,)), dma((4,)), dma((4,)), dma((4,)), dma((4,)), dma((4,)), dma((4,)), dma((4,)),
+            dma((2,)), dma((4,)), dma((4,)), dma((4,)), dma((4,)), dma((6,)), dma((6,)), dma((6,)), dma((6,)),
             dma((4,)), dma((4,)), dma((4,)), dma((4,)), dma((BLK,)), dma((BLK,)),
             dma((INT,)), dma((INT,)), dma((INT,)), dma((INT,)),
         ],

time: 79.4 us -> 75.1 us (0.946)
  local copies, waits for them, and re-layouts: 8.35 us -> 4.8 us
  Pallas kernels: 68 us -> 66.7 us
    pallas_call x1, Pallas kernels: 68 us -> 66.7 us  [per_device(): pl.pallas_call(kernel, out_shape=jax.ShapeDtypeStruct((ROWS, 256), F32),...]
where the time goes in v4:
time: 75.1 us; the launch traced here: 74.2 us
  Pallas kernels  66.7 us (89%)
  local copies, waits for them, and re-layouts  4.8 us (6%)
  other arithmetic  2.44 us (3%)
    pallas_call x1, Pallas kernels, per_device(): pl.pallas_call(kernel, out_shape=jax.ShapeDtypeStruct((ROWS, 256), F32),...  66.7 us

profile of v4, /device:TPU:1, one launch (start us, length us, event | category | flops | bytes accessed | tf_op | source)
XLA Modules:
  0.0 74.2 jit_solution(8277273495242032704)
XLA Ops:
  0.0 0.0 copy-start.1
  0.0 1.0 %select_reduce_fusion = (s32[4]{0:T(128)S(1)}, s32[4]{0:T(128)S(1)}, s32[4]{0:T(128)S(1)}) fusion(s32[4]{0:T(128)} %param.10, s32[64]{0:T(128)} %param.8, s32[4]{0:T(128)} %param.11, s32[4]{0:T(128)S(1)} %iota_add_fusion), kind=kLoop, calls=%fused_computation.9 | loop fusion | flops 2292 | bytes 352 | tf_op jit(solution)/shard_map/reduce_sum | solution.py:31
  1.0 0.1 broadcast_xor_fusion.2
  1.1 0.1 xor.152
  1.1 0.7 broadcast_and_fusion
  1.8 0.1 dynamic_slice.9
  1.9 0.1 dynamic_slice.11
  2.0 0.1 broadcast_xor_fusion.1
  2.1 0.1 xor.162
  2.2 0.3 convert_reduce_fusion
  2.5 0.1 dynamic-slice_multiply_fusion
  2.5 0.1 xor_add_fusion.1
  2.6 0.1 add.112
  2.7 0.1 broadcast_xor_fusion
  2.8 0.1 reshape.275
  2.9 0.1 add.103
  3.0 0.1 xor.146
  3.1 0.1 reshape.271
  3.2 0.1 reshape.273
  3.3 0.1 copy.24
  3.4 0.1 copy.23
  3.5 0.1 reshape.272.placed_ref
  3.7 0.1 xor_add_fusion
  3.8 0.1 copy.34
  3.8 0.1 reshape.277
  4.0 0.1 reshape.278
  4.1 0.1 reshape.279
  4.2 0.1 copy.32.siac_ref
  4.3 0.1 xor.143
  4.4 0.1 xor.144
  4.5 0.1 copy.28.skbj_ref
  4.6 0.1 reshape.284.skiac_ref
  4.8 0.2 reshape.285.irrc_ref
  4.9 0.0 copy-done.1
  4.9 0.1 copy.33
  5.0 0.1 pad.44.clone
  5.1 0.4 copy.31.column_ref
  5.5 0.0 copy-start
  5.6 1.1 %copy-done = f32[4,608,4,19]{1,2,3,0:T(4,128)S(1)} copy-done((f32[4,608,4,19]{1,2,3,0:T(4,128)S(1)}, f32[4,608,4,19]{1,2,3,0:T(4,128)}, u32[]{:S(2)}) %copy-start) | copy-done | bytes 739352
  6.7 66.7 %shard_map.64 = f32[80,256]{1,0:T(8,128)S(1)} custom-call(f32[4,19,4,608]{3,2,1,0:T(4,128)S(1)} %bitcast.26, s32[4,80,1]{2,1,0:T(8,128)S(1)} %copy.28.skbj_ref, f32[384,608]{1,0:T(8,128)S(1)} %bitcast.25, s32[384,1]{1,0:T(8,128)S(1)} %reshape.284.skiac_ref, s32[1,608]{1,0:T(1,128)S(1)} %reshape.269.virt_ref, s32[1,608]{1,0:T(1,128)S(1)} %reshape.270.place_ref, ...), custom_call_target="tpu_custom_call" | custom-call | tf_op jit(solution)/shard_map/pallas_call | solution.py:389
  73.4 0.8 %reshape.283 = f32[4,19,4,38]{3,2,1,0:T(4,128)} reshape(f32[76,152]{1,0:T(8,128)S(1)} %bitcast.27) | data formatting | bytes 92416 | tf_op jit(solution)/shard_map/reshape | solution.py:421
  (28 shorter events, 0.2 us)
Async XLA Ops:
  0.0 4.9 %copy-start.1 = (f32[4,19,4,608]{3,2,1,0:T(4,128)S(1)}, f32[4,19,4,608]{3,2,1,0:T(4,128)}, u32[]{:S(2)}) copy-start(f32[4,19,4,608]{3,2,1,0:T(4,128)} %param.6) | copy-start | bytes 2217988
  5.5 1.1 %copy-start = (f32[4,608,4,19]{1,2,3,0:T(4,128)S(1)}, f32[4,608,4,19]{1,2,3,0:T(4,128)}, u32[]{:S(2)}) copy-start(f32[4,608,4,19]{1,2,3,0:T(4,128)} %param.7) | copy-start | bytes 2217988

commit v5 on v4

--- a/solution.py
+++ b/solution.py
@@ -1,5 +1,6 @@
 import jax
 import jax.numpy as jnp
+import numpy as np
 from jax import lax
 from jax.experimental import pallas as pl
 from jax.experimental.pallas import tpu as pltpu
@@ -25,12 +26,6 @@
 PITCH = 21
 
 
-def lookup(labels, where_at):
-    positions = jnp.arange(labels.shape[0], dtype=jnp.int32)
-    onehot = (where_at[:, None] == positions[None, :]).astype(jnp.int32)
-    return jnp.sum(onehot * labels[None, :], axis=1)
-
-
 def halves(x):
     high = x.astype(BF16)
     return high, (x - high.astype(F32)).astype(BF16)
@@ -45,10 +40,9 @@
 
 
 def kernel(
-    int_ref, skbj_ref, a_ref, skiac_ref, virt_ref, place_ref, placed_ref, irrc_ref, skia_ref, row_ref, column_ref, sia_ref,
-    rowz_ref, siac_ref,
+    int_ref, a_ref, virt_ref, index_ref, pair_ref, occ_ref, i_ref, j_ref,
     out_ref,
-    g_ref, g_rows, gh0, gh1, spaced, moved, dbuf, arrived, ebuf, acc, zsend, zrecv, ysum, ygath,
+    g_ref, g_rows, column_buf, gh0, gh1, spaced, moved, dbuf, arrived, ebuf, acc, zsend, zrecv, ysum, ygath,
     own_sem, p0_send, p0_recv, p1_send, p1_recv, q0_send, q0_recv, q1_send, q1_recv,
     s0_send, s0_recv, s1_send, s1_recv, d_send, d_recv, z_send, z_recv, y_send, y_recv,
 ):
@@ -84,18 +78,53 @@
     own0 = pltpu.make_async_copy(g_ref.at[pl.ds(0, HALF)], gh0.at[cy, core, cx], own_sem.at[0])
     own1 = pltpu.make_async_copy(g_ref.at[pl.ds(HALF, HALF)], gh1.at[cx, core, cy], own_sem.at[1])
 
+    irr_i = [occ_ref[i_ref[i]] for i in range(NI)]
+    irr_j = [occ_ref[j_ref[j]] for j in range(NJ)]
+    occ_k = [occ_ref[mz * NK + k] for k in range(NK)]
+    virt = virt_ref[...]
+
+    label = lax.broadcasted_iota(jnp.int32, (16, NV), 0)
+    mine = jnp.where(label == virt, 1.0, 0.0)
+    earlier = lax.broadcasted_iota(jnp.int32, (NV, NV), 0) < lax.broadcasted_iota(jnp.int32, (NV, NV), 1)
+    counts = nn(mine.astype(BF16), jnp.where(earlier, 1.0, 0.0).astype(BF16))
+    place = jnp.sum(mine * counts, axis=0, keepdims=True)
+    both = jnp.where(label == 0, virt.astype(F32), jnp.where(label == 1, place, 0.0)).astype(BF16)
+
+    def look(index):
+        chosen = lax.broadcasted_iota(jnp.int32, (NV, index.shape[1]), 0) == index
+        found = nn(both, jnp.where(chosen, 1.0, 0.0).astype(BF16))
+        return found[0:1].astype(jnp.int32), found[1:2].astype(jnp.int32)
+
+    def pick(values, which):
+        out = jnp.zeros_like(which)
+        for n, value in enumerate(values):
+            out = jnp.where(which == n, value, out)
+        return out
+
+    def turn(row):
+        return jnp.broadcast_to(row.astype(F32), (8, row.shape[1])).T[:, 0:1].astype(jnp.int32)
+
+    def constant(n, lanes):
+        return index_ref[n:n + 1, 0:lanes]
+
+    def own_label(n, lanes):
+        offset = constant(n, lanes)
+        return offset >= 0, look(me * NA + offset)[0]
+
     def onehot(places):
         row = lax.broadcasted_iota(jnp.int32, (CAP, places.shape[1]), 0)
         return jnp.where(row == places, 1.0, 0.0).astype(BF16)
 
-    p_all = onehot(place_ref[...])
+    p_all = onehot(place.astype(jnp.int32))
+    valid, s_bj = own_label(5, 128)
+    s_bj = jnp.bitwise_xor(s_bj, pick(irr_j, constant(6, 128)))
     for k in range(NK):
         for b in range(NA):
             g_rows[k, b * NJ:(b + 1) * NJ] = int_ref[k, b]
         g_rows[k, NA * NJ:] = jnp.zeros((ROWS - NA * NJ, NV), F32)
     packed = []
     for k in range(NK):
-        high, low = halves(jnp.where(skbj_ref[k] == virt_ref[...], g_rows[k], 0.0))
+        high, low = halves(jnp.where(turn(jnp.where(valid, jnp.bitwise_xor(s_bj, occ_k[k]), -2))[:ROWS] == virt, g_rows[k], 0.0))
         packed.append(nt(high, p_all) + nt(low, p_all))
     g_ref[...] = jnp.concatenate(packed, axis=1)
     pl.semaphore_wait(barrier, BLK - 1 + INT - 1)
@@ -207,11 +236,35 @@
     @pl.loop(0, 8)
     def _(n):
         row = lax.broadcasted_iota(jnp.int32, (NJ * CAP, GROUP), 0)
-        ebuf[n] = jnp.where(row == row_ref[n] // 8, 1.0, 0.0).astype(BF16)
-
-    high, low = halves(jnp.where(skiac_ref[...] == virt_ref[...], a_ref[...], 0.0))
+        orbital = pair_ref[n, 0:1]
+        which = pair_ref[n, 1:2]
+        irrep, at = look(orbital)
+        at = jnp.where(orbital >= 0, at + CAP * which, -1)
+        ebuf[n] = jnp.where(row == at[:, :GROUP], 1.0, 0.0).astype(BF16)
+        column_buf[n] = turn(jnp.bitwise_xor(irrep, pick(irr_j, which)))[:GROUP]
+
+    def s_kia(n):
+        good, irrep = own_label(n, 384)
+        m = constant(n + 1, 384)
+        irrep = jnp.bitwise_xor(irrep, pick([irr_i[i] for k in range(NK) for i in range(NI)], m))
+        irrep = jnp.bitwise_xor(irrep, pick([occ_k[k] for k in range(NK) for i in range(NI)], m))
+        return jnp.where(good, irrep, -2)
+
+    high, low = halves(jnp.where(turn(s_kia(1)) == virt, a_ref[...], 0.0))
     direct = nt(p_all, high) + nt(p_all, low)
-    p_t = onehot(placed_ref[...])
+    orbital = constant(0, BLK * CPAD)
+    irrep, at = look(orbital)
+    p_t = onehot(jnp.where(orbital >= 0, at, -1))
+    irrep_c = turn(jnp.where(orbital >= 0, irrep, -1))
+    s_row = s_kia(3)
+    good, s_ia = own_label(7, 128)
+    s_ia = jnp.where(good, jnp.bitwise_xor(s_ia, pick(irr_i, constant(8, 128))), -2)
+    s_ia_column = turn(s_ia)[:ROWS]
+    offset = constant(9, 256)
+    which = constant(10, 256)
+    s_jb, at_z = look(mz * NB + offset)
+    s_jb = jnp.where(offset >= 0, jnp.bitwise_xor(s_jb, pick(irr_j, which)), -1)
+    at_z = jnp.where(offset >= 0, at_z + CAP * which, -1)
 
     def d_wait(n):
         d = (me + n) % BLK
@@ -220,7 +273,7 @@
     each(1, BLK, d_wait)
     for d in range(BLK):
         arrived[d * CPAD:d * CPAD + NA] = dbuf[d]
-    swapped = jnp.where(irrc_ref[...] == skia_ref[...], arrived[...], 0.0)
+    swapped = jnp.where(irrep_c == s_row, arrived[...], 0.0)
     s_high, s_low = halves(swapped)
     s_t = nn(p_t, s_high) + nn(p_t, s_low)
     columns = []
@@ -239,7 +292,7 @@
     def product(piece, n):
         g_high, g_low = halves(piece.reshape(GROUP, NK * CAP))
         r = nn(g_high, w_high) + (nn(g_high, w_low) + nn(g_low, w_high))
-        r_high, r_low = halves(jnp.where(column_ref[n] % 8 == sia_ref[...], r, 0.0))
+        r_high, r_low = halves(jnp.where(column_buf[n] == s_ia, r, 0.0))
         acc[...] += nn(ebuf[n], r_high) + nn(ebuf[n], r_low)
 
     def product0(n):
@@ -305,14 +358,14 @@
         y_copy(n).start()
     ygath[mz] = total
     row = lax.broadcasted_iota(jnp.int32, (NJ * CAP, 256), 0)
-    spread = jnp.where(row == rowz_ref[...] // 8, 1.0, 0.0).astype(BF16)
+    spread = jnp.where(row == at_z, 1.0, 0.0).astype(BF16)
     each(1, INT, lambda n: y_copy(n).wait_recv())
     whole = jnp.concatenate(
         [jnp.concatenate([ygath[block * 5 + group] for group in range(5)], axis=0) for block in range(3)], axis=1
     )
     y_high, y_low = halves(whole)
     out = nn(y_high, spread) + nn(y_low, spread)
-    out_ref[...] = jnp.where(siac_ref[...] == rowz_ref[...] % 8, out, 0.0)
+    out_ref[...] = jnp.where(s_ia_column == s_jb, out, 0.0)
 
     each(1, 4, lambda o: p0(o).wait_send())
     each(1, 4, lambda o: p1(o).wait_send())
@@ -335,65 +388,54 @@
     return jnp.pad(x, [(0, n - m) for n, m in zip(shape, x.shape)], constant_values=value)
 
 
-def blocks_of_six(x, value):
-    x = pad_to(x, (x.shape[0], 18, PITCH), value).reshape(-1, 3, 6 * PITCH)
-    return pad_to(x, (x.shape[0], 3, 128), value).reshape(-1, 384)
-
-
-def by_group(x):
-    x = x.reshape(4, 4, 2, 2, HALF)
-    first = jnp.transpose(x[:, :, :, 0], (0, 2, 1, 3)).reshape(4, GROUP)
-    second = jnp.transpose(x[:, :, :, 1], (1, 2, 0, 3)).reshape(4, GROUP)
-    return jnp.concatenate([first, second], axis=0)
+def index_tables():
+    far = -100000
+    table = np.full((16, BLK * CPAD), far, np.int32)
+    lane = np.arange(BLK * CPAD)
+    table[0] = np.where(lane % CPAD < NA, NA * (lane // CPAD) + lane % CPAD, -1)
+    lane = np.arange(384)
+    table[1, :384] = np.where(lane % CPAD < NA, lane % CPAD, far)
+    table[2, :384] = lane // CPAD
+    m = 6 * (lane // 128) + lane % 128 // PITCH
+    a = lane % 128 % PITCH
+    table[3, :384] = np.where((a < NA) & (lane % 128 < 6 * PITCH) & (m < NI * NK), a, far)
+    table[4, :384] = m
+    lane = np.arange(NA * NJ)
+    table[5, :NA * NJ] = lane // NJ
+    table[6, :NA * NJ] = lane % NJ
+    table[7, :NI * NA] = lane % NA
+    table[8, :NI * NA] = lane // NA
+    lane = np.arange(NJ * NB)
+    table[9, :NJ * NB] = lane % NB
+    table[10, :NJ * NB] = lane // NB
+    pairs = np.full((8, 2, 384), -1, np.int32)
+    lane = np.arange(GROUP)
+    core, other, row = lane // (4 * HALF), lane // HALF % 4, lane % HALF
+    for n in range(8):
+        y, x = (n, other) if n < 4 else (other, n - 4)
+        n_row = row + HALF * (n // 4)
+        good = n_row < NA * NJ
+        pairs[n, 0, :GROUP] = np.where(good, ((y * 4 + x) * 2 + core) * NA + n_row // NJ, -1)
+        pairs[n, 1, :GROUP] = n_row % NJ
+    return table, pairs
 
 
 def per_device(amplitudes, integrals, occ_irrep, virt_irrep, i_batch, j_batch):
-    blk = lax.axis_index("blk")
-    z = lax.axis_index("int")
-    occ_k = lookup(occ_irrep, z * NK + jnp.arange(NK, dtype=jnp.int32))
-    virt_irrep = lax.optimization_barrier(jnp.bitwise_and(virt_irrep, 7))
-    virt_a = lax.dynamic_slice_in_dim(virt_irrep, blk * NA, NA)
-    irr_i = lookup(occ_irrep, i_batch)
-    irr_j = lookup(occ_irrep, j_batch)
-    orbital = jnp.arange(NV, dtype=jnp.int32)
-    alike = (virt_irrep[:, None] == virt_irrep[None, :]) & (orbital[None, :] < orbital[:, None])
-    place = jnp.sum(alike.astype(jnp.int32), axis=1)
-    s_ika = jnp.bitwise_xor(
-        jnp.bitwise_xor(irr_i[:, None, None], occ_k[None, None, :]), virt_a[None, :, None]
-    )
     a_rows = pad_to(jnp.transpose(amplitudes, (2, 0, 1, 3)), (NK, NI, CPAD, NV)).reshape(NK * NI * CPAD, NV)
-    s_kia = jnp.transpose(s_ika, (2, 0, 1)).reshape(1, NK * NI, NA)
-    s_kia_column = pad_to(s_kia, (1, NK * NI, CPAD), -2).reshape(NK * NI * CPAD, 1)
-    s_kia = blocks_of_six(s_kia, -2)
-
     ints = jnp.transpose(integrals, (0, 3, 2, 1))
-    s_kbj = jnp.bitwise_xor(
-        jnp.bitwise_xor(occ_k[:, None, None], virt_a[None, :, None]), irr_j[None, None, :]
-    )
-    s_kbj = pad_to(s_kbj.reshape(NK, NA * NJ), (NK, ROWS), -2).reshape(NK, ROWS, 1)
-
-    placed = pad_to(place.reshape(BLK, NA), (BLK, CPAD), -1).reshape(1, BLK * CPAD)
-    irr_c = pad_to(virt_irrep.reshape(BLK, NA), (BLK, CPAD), -1).reshape(BLK * CPAD, 1)
-    s_ia = jnp.bitwise_xor(irr_i[:, None], virt_a[None, :]).reshape(1, NI * NA)
-
-    offset = 8 * CAP * jnp.arange(NJ, dtype=jnp.int32)
-    pairs = 8 * place[:, None] + offset[None, :] + jnp.bitwise_xor(virt_irrep[:, None], irr_j[None, :])
-    pairs = by_group(pad_to(pairs.reshape(BLK, NA * NJ), (BLK, ROWS), -1))
-    virt_b = lax.dynamic_slice_in_dim(virt_irrep, z * NB, NB)
-    place_b = lax.dynamic_slice_in_dim(place, z * NB, NB)
-    row_z = 8 * place_b[None, :] + offset[:, None] + jnp.bitwise_xor(irr_j[:, None], virt_b[None, :])
-    row_z = pad_to(row_z.reshape(1, NJ * NB), (1, 256), -1)
+    table, pairs = index_tables()
 
     vmem = pl.BlockSpec(memory_space=pltpu.VMEM)
     dma = pltpu.SemaphoreType.DMA
     out = pl.pallas_call(
         kernel,
         out_shape=jax.ShapeDtypeStruct((ROWS, 256), F32),
-        in_specs=[vmem] * 14,
+        in_specs=[vmem] * 5 + [pl.BlockSpec(memory_space=pltpu.SMEM)] * 3,
         out_specs=vmem,
         scratch_shapes=[
             pltpu.VMEM((ROWS, NK * CAP), F32),
             pltpu.VMEM((NK, ROWS, NV), F32),
+            pltpu.VMEM((8, GROUP, 1), jnp.int32),
             pltpu.VMEM((4, 2, 4, HALF, NK * CAP), F32),
             pltpu.VMEM((4, 2, 4, HALF, NK * CAP), F32),
             pltpu.VMEM((NI * NK * CPAD, 1024), F32),
@@ -414,9 +456,7 @@
             collective_id=0, has_side_effects=True, vmem_limit_bytes=48 * 1024 * 1024
         ),
     )(
-        ints, s_kbj, a_rows, s_kia_column, virt_irrep.reshape(1, NV), place.reshape(1, NV), placed, irr_c, s_kia,
-        pairs.reshape(8, 1, GROUP), pairs.reshape(8, GROUP, 1), pad_to(s_ia, (1, 128), -2), row_z,
-        pad_to(s_ia, (1, ROWS), -2).reshape(ROWS, 1),
+        ints, a_rows, virt_irrep.reshape(1, NV), jnp.asarray(table), jnp.asarray(pairs), occ_irrep, i_batch, j_batch
     )
     return out[:NI * NA, :NJ * NB].reshape(NI, NA, NJ, NB)
 

time: 75.1 us -> 71.6 us (0.953)
  other arithmetic: 2.44 us -> 0 us
  local copies, waits for them, and re-layouts: 4.8 us -> 3.4 us
  Pallas kernels: 66.7 us -> 67.5 us
    reshape x17 -> x0, local copies, waits for them, and re-layouts: 1.68 us -> none  [the longest x1 0.43 us: per_device(): pairs.reshape(8, GROUP, 1)]
    reduce_sum x2 -> x0, other arithmetic: 1.26 us -> none  [the longest x1 0.97 us: lookup(): return jnp.sum(onehot * labels[None, :], axis=1)]
    unnamed x8 -> x15, local copies, waits for them, and re-layouts: 1.3 us -> 2.53 us
    pallas_call x1, Pallas kernels: 66.7 us -> 67.5 us  [per_device(): pl.pallas_call(kernel, out_shape=jax.ShapeDtypeStruct((ROWS, 256), F32),...]
where the time goes in v5:
time: 71.6 us; the launch traced here: 71 us
  Pallas kernels  67.5 us (94%)
  local copies, waits for them, and re-layouts  3.4 us (5%)
    pallas_call x1, Pallas kernels, per_device(): pl.pallas_call(kernel, out_shape=jax.ShapeDtypeStruct((ROWS, 256), F32),...  67.5 us
    unnamed x15, local copies, waits for them, and re-layouts  2.53 us

profile of v5, /device:TPU:1, one launch (start us, length us, event | category | flops | bytes accessed | tf_op | source)
XLA Modules:
  0.0 71.0 jit_solution(7387076272028403497)
XLA Ops:
  0.0 1.2 %copy.11 = f32[4,4,19,608]{3,2,1,0:T(8,128)S(1)} copy(f32[4,4,19,608]{3,0,2,1:T(4,128)} %bitcast.7) | data formatting | bytes 1478656
  1.2 0.0 copy-start.6
  1.2 0.0 copy-start
  1.2 0.0 copy-start.1
  1.2 0.0 copy-start.2
  1.3 0.1 pad.4.clone
  1.3 0.6 copy-done.6
  1.9 0.0 copy-start.3
  1.9 0.0 copy-start.4
  1.9 0.0 copy-start.5
  1.9 0.4 copy-done
  2.4 0.0 copy-done.1
  2.4 0.0 copy-done.2
  2.4 0.3 copy-done.3
  2.6 0.0 copy-done.4
  2.6 0.0 copy-done.5
  2.7 67.5 %shard_map.82 = f32[80,256]{1,0:T(8,128)S(1)} custom-call(f32[4,19,4,608]{3,2,1,0:T(4,128)S(1)} %bitcast.5, f32[384,608]{1,0:T(8,128)S(1)} %bitcast.4, s32[1,608]{1,0:T(1,128)S(1)} %reshape.10.virt_ref, s32[16,768]{1,0:T(8,128)S(1)} %copy-done.1, s32[8,2,384]{2,1,0:T(2,128)S(1)} %copy-done.2, s32[64]{0:T(128)S(1)} %copy-done.3, s32[4]{0:T(128)S(1)} %copy-done.4, ...), custom_call_target="tpu_custom_call" | custom-call | tf_op jit(solution)/shard_map/pallas_call | solution.py:430
  70.2 0.8 %reshape.11 = f32[4,19,4,38]{3,2,1,0:T(4,128)} reshape(f32[76,152]{1,0:T(8,128)S(1)} %bitcast.6) | data formatting | bytes 92416 | tf_op jit(solution)/shard_map/reshape | solution.py:461
  (1 shorter events, 0.0 us)
Async XLA Ops:
  1.2 0.7 copy-start.6
  1.2 1.1 %copy-start = (f32[4,608,4,19]{1,2,3,0:T(4,128)S(1)}, f32[4,608,4,19]{1,2,3,0:T(4,128)}, u32[]{:S(2)}) copy-start(f32[4,608,4,19]{1,2,3,0:T(4,128)} %param.9) | copy-start | bytes 2217988
  1.2 1.1 %copy-start.1 = (s32[16,768]{1,0:T(8,128)S(1)}, s32[16,768]{1,0:T(8,128)}, u32[]{:S(2)}) copy-start(s32[16,768]{1,0:T(8,128)} %constant.7.clone.index_ref) | copy-start | bytes 147460
  1.2 1.1 %copy-start.2 = (s32[8,2,384]{2,1,0:T(2,128)S(1)}, s32[8,2,384]{2,1,0:T(2,128)}, u32[]{:S(2)}) copy-start(s32[8,2,384]{2,1,0:T(2,128)} %constant.8.clone.pair_ref) | copy-start | bytes 73732
  1.9 0.7 %copy-start.3 = (s32[64]{0:T(128)S(1)}, s32[64]{0:T(128)}, u32[]{:S(2)}) copy-start(s32[64]{0:T(128)} %occ_ref.1) | copy-start | bytes 772
  1.9 0.7 %copy-start.4 = (s32[4]{0:T(128)S(1)}, s32[4]{0:T(128)}, u32[]{:S(2)}) copy-start(s32[4]{0:T(128)} %i_ref.1) | copy-start | bytes 52
  1.9 0.7 %copy-start.5 = (s32[4]{0:T(128)S(1)}, s32[4]{0:T(128)}, u32[]{:S(2)}) copy-start(s32[4]{0:T(128)} %j_ref.1) | copy-start | bytes 52

commit v6 on v5

--- a/solution.py
+++ b/solution.py
@@ -166,6 +166,8 @@
         at = pl.ds(pl.multiple_of(tile * 128, 128), 128)
         blocks = [spaced[m * CPAD:(m + 1) * CPAD, at] for m in range(NI * NK)]
         for part in range(4):
+            d = 4 * tile + part
+            lasts = []
             for t in range(3):
                 held = jnp.zeros((CPAD, 128), F32)
                 here = blocks[6 * t:6 * t + 6]
@@ -173,7 +175,16 @@
                     shift = (PITCH * n - 32 * part) % 128
                     turned = pltpu.roll(block, shift, 1) if shift else block
                     held = jnp.where((small >= PITCH * n) & (small < PITCH * n + NA), turned, held)
-                moved[4 * tile + part, :, t * 128:(t + 1) * 128] = held[:NA]
+                last = held[16:]
+                if t == 2:
+                    packed_rows = jnp.concatenate([pltpu.roll(last, 84, 1)[:3], pltpu.roll(last, 42, 1)[:5]], axis=0)
+                    top = jnp.where(small[:8] >= 84, packed_rows, held[:8])
+                    moved[d, 32:40] = top
+                    moved[d, 40:48] = held[8:16]
+                else:
+                    moved[d, 16 * t:16 * t + 16] = held[:16]
+                    lasts.append(last)
+            moved[d, 48:56] = jnp.concatenate([lasts[0][:3], lasts[1][:5]], axis=0)
 
         @pl.when(step > 0)
         def _():
@@ -271,8 +282,18 @@
         remote(moved.at[d], dbuf.at[d], d_send.at[d], d_recv.at[d], (d, mz)).wait_recv()
 
     each(1, BLK, d_wait)
-    for d in range(BLK):
-        arrived[d * CPAD:d * CPAD + NA] = dbuf[d]
+    @pl.loop(0, BLK)
+    def _(d):
+        first = pl.multiple_of(d * CPAD, 8)
+        for t in range(3):
+            arrived[pl.ds(first, 16), t * 128:(t + 1) * 128] = dbuf[d, 16 * t:16 * t + 16]
+        rest = dbuf[d, 48:56]
+        arrived[pl.ds(first + 16, 8), 0:128] = rest
+        arrived[pl.ds(first + 16, 8), 128:256] = jnp.concatenate([rest[3:6], rest[:5]], axis=0)
+        top = dbuf[d, 32:40]
+        below = jnp.concatenate([pltpu.roll(top, 86, 1)[3:6], top[:5]], axis=0)
+        arrived[pl.ds(first + 16, 8), 256:384] = jnp.where(small[:8] < 2 * PITCH, pltpu.roll(top, 44, 1), below)
+
     swapped = jnp.where(irrep_c == s_row, arrived[...], 0.0)
     s_high, s_low = halves(swapped)
     s_t = nn(p_t, s_high) + nn(p_t, s_low)
@@ -332,13 +353,17 @@
 
     lax.fori_loop(0, 4, products, 0)
 
-    def z_copy(n):
+    def z_copy(n, half):
         target = (mz + n) % INT
-        return remote(zsend.at[target], zrecv.at[mz], z_send.at[n], z_recv.at[n], (me, target))
-
-    def y_copy(n):
+        rows = pl.ds(8 * half, 8)
+        sem = INT * half + n
+        return remote(zsend.at[target, rows], zrecv.at[mz, rows], z_send.at[sem], z_recv.at[sem], (me, target))
+
+    def y_copy(n, half):
         target = (mz + n) % INT
-        return remote(ysum, ygath.at[mz], y_send.at[n], y_recv.at[n], (me, target))
+        rows = pl.ds(8 * half, 8)
+        sem = INT * half + n
+        return remote(ysum.at[rows], ygath.at[mz, rows], y_send.at[sem], y_recv.at[sem], (me, target))
 
     turned = acc[...].T[:ROWS]
     for block in range(3):
@@ -346,20 +371,24 @@
             zsend[block * 5 + group] = turned[group * 16:(group + 1) * 16, block * 128:(block + 1) * 128]
     zsend[15] = jnp.zeros((16, 128), F32)
 
-    for n in FAR_FIRST:
-        z_copy(n).start()
+    for half in range(2):
+        for n in FAR_FIRST:
+            z_copy(n, half).start()
     zrecv[mz] = zsend[mz]
-    each(1, INT, lambda n: z_copy(n).wait_recv())
-    total = zrecv[0]
-    for n in range(1, INT):
-        total = total + zrecv[n]
-    ysum[...] = total
-    for n in FAR_FIRST:
-        y_copy(n).start()
-    ygath[mz] = total
+    for half in range(2):
+        each(1, INT, lambda n: z_copy(n, half).wait_recv())
+        rows = pl.ds(8 * half, 8)
+        total = zrecv[0, rows]
+        for n in range(1, INT):
+            total = total + zrecv[n, rows]
+        ysum[rows] = total
+        for n in FAR_FIRST:
+            y_copy(n, half).start()
+        ygath[mz, rows] = total
     row = lax.broadcasted_iota(jnp.int32, (NJ * CAP, 256), 0)
     spread = jnp.where(row == at_z, 1.0, 0.0).astype(BF16)
-    each(1, INT, lambda n: y_copy(n).wait_recv())
+    for half in range(2):
+        each(1, INT, lambda n: y_copy(n, half).wait_recv())
     whole = jnp.concatenate(
         [jnp.concatenate([ygath[block * 5 + group] for group in range(5)], axis=0) for block in range(3)], axis=1
     )
@@ -380,8 +409,9 @@
         s0(n).wait_send()
         s1(n).wait_send()
     each(1, BLK, lambda n: d_copy((me + n) % BLK).wait_send())
-    each(1, INT, lambda n: z_copy(n).wait_send())
-    each(1, INT, lambda n: y_copy(n).wait_send())
+    for half in range(2):
+        each(1, INT, lambda n: z_copy(n, half).wait_send())
+        each(1, INT, lambda n: y_copy(n, half).wait_send())
 
 
 def pad_to(x, shape, value=0):
@@ -439,8 +469,8 @@
             pltpu.VMEM((4, 2, 4, HALF, NK * CAP), F32),
             pltpu.VMEM((4, 2, 4, HALF, NK * CAP), F32),
             pltpu.VMEM((NI * NK * CPAD, 1024), F32),
-            pltpu.VMEM((BLK, NA, 384), F32),
-            pltpu.VMEM((BLK, NA, 384), F32),
+            pltpu.VMEM((BLK, 56, 128), F32),
+            pltpu.VMEM((BLK, 56, 128), F32),
             pltpu.VMEM((BLK * CPAD, 384), F32),
             pltpu.VMEM((8, NJ * CAP, GROUP), BF16),
             pltpu.VMEM((NJ * CAP, 128), F32),
@@ -450,7 +480,7 @@
             pltpu.VMEM((INT, 16, 128), F32),
             dma((2,)), dma((4,)), dma((4,)), dma((4,)), dma((4,)), dma((6,)), dma((6,)), dma((6,)), dma((6,)),
             dma((4,)), dma((4,)), dma((4,)), dma((4,)), dma((BLK,)), dma((BLK,)),
-            dma((INT,)), dma((INT,)), dma((INT,)), dma((INT,)),
+            dma((2 * INT,)), dma((2 * INT,)), dma((2 * INT,)), dma((2 * INT,)),
         ],
         compiler_params=pltpu.CompilerParams(
             collective_id=0, has_side_effects=True, vmem_limit_bytes=48 * 1024 * 1024

time: 71.6 us -> 69.5 us (0.971)
  Pallas kernels: 67.5 us -> 65.7 us
    pallas_call x1, Pallas kernels: 67.5 us -> 65.7 us  [per_device(): pl.pallas_call(kernel, out_shape=jax.ShapeDtypeStruct((ROWS, 256), F32),...]
where the time goes in v6:
time: 69.5 us; the launch traced here: 69.2 us
  Pallas kernels  65.7 us (95%)
  local copies, waits for them, and re-layouts  3.4 us (5%)
    pallas_call x1, Pallas kernels, per_device(): pl.pallas_call(kernel, out_shape=jax.ShapeDtypeStruct((ROWS, 256), F32),...  65.7 us
    unnamed x15, local copies, waits for them, and re-layouts  2.53 us

profile of v6, /device:TPU:1, one launch (start us, length us, event | category | flops | bytes accessed | tf_op | source)
XLA Modules:
  0.0 69.2 jit_solution(32742452463925749)
XLA Ops:
  0.0 1.2 %copy.11 = f32[4,4,19,608]{3,2,1,0:T(8,128)S(1)} copy(f32[4,4,19,608]{3,0,2,1:T(4,128)} %bitcast.7) | data formatting | bytes 1478656
  1.2 0.0 copy-start.6
  1.2 0.0 copy-start
  1.2 0.0 copy-start.1
  1.2 0.0 copy-start.2
  1.3 0.1 pad.4.clone
  1.3 0.6 copy-done.6
  1.9 0.0 copy-start.3
  1.9 0.0 copy-start.4
  1.9 0.0 copy-start.5
  1.9 0.4 copy-done
  2.4 0.0 copy-done.1
  2.4 0.0 copy-done.2
  2.4 0.3 copy-done.3
  2.6 0.0 copy-done.4
  2.6 0.0 copy-done.5
  2.7 65.7 %shard_map.82 = f32[80,256]{1,0:T(8,128)S(1)} custom-call(f32[4,19,4,608]{3,2,1,0:T(4,128)S(1)} %bitcast.5, f32[384,608]{1,0:T(8,128)S(1)} %bitcast.4, s32[1,608]{1,0:T(1,128)S(1)} %reshape.10.virt_ref, s32[16,768]{1,0:T(8,128)S(1)} %copy-done.1, s32[8,2,384]{2,1,0:T(2,128)S(1)} %copy-done.2, s32[64]{0:T(128)S(1)} %copy-done.3, s32[4]{0:T(128)S(1)} %copy-done.4, ...), custom_call_target="tpu_custom_call" | custom-call | tf_op jit(solution)/shard_map/pallas_call | solution.py:460
  68.4 0.8 %reshape.11 = f32[4,19,4,38]{3,2,1,0:T(4,128)} reshape(f32[76,152]{1,0:T(8,128)S(1)} %bitcast.6) | data formatting | bytes 92416 | tf_op jit(solution)/shard_map/reshape | solution.py:491
  (1 shorter events, 0.0 us)
Async XLA Ops:
  1.2 0.7 copy-start.6
  1.2 1.1 %copy-start = (f32[4,608,4,19]{1,2,3,0:T(4,128)S(1)}, f32[4,608,4,19]{1,2,3,0:T(4,128)}, u32[]{:S(2)}) copy-start(f32[4,608,4,19]{1,2,3,0:T(4,128)} %param.9) | copy-start | bytes 2217988
  1.2 1.1 %copy-start.1 = (s32[16,768]{1,0:T(8,128)S(1)}, s32[16,768]{1,0:T(8,128)}, u32[]{:S(2)}) copy-start(s32[16,768]{1,0:T(8,128)} %constant.7.clone.index_ref) | copy-start | bytes 147460
  1.2 1.1 %copy-start.2 = (s32[8,2,384]{2,1,0:T(2,128)S(1)}, s32[8,2,384]{2,1,0:T(2,128)}, u32[]{:S(2)}) copy-start(s32[8,2,384]{2,1,0:T(2,128)} %constant.8.clone.pair_ref) | copy-start | bytes 73732
  1.9 0.7 %copy-start.3 = (s32[64]{0:T(128)S(1)}, s32[64]{0:T(128)}, u32[]{:S(2)}) copy-start(s32[64]{0:T(128)} %occ_ref.1) | copy-start | bytes 772
  1.9 0.7 %copy-start.4 = (s32[4]{0:T(128)S(1)}, s32[4]{0:T(128)}, u32[]{:S(2)}) copy-start(s32[4]{0:T(128)} %i_ref.1) | copy-start | bytes 52
  1.9 0.7 %copy-start.5 = (s32[4]{0:T(128)S(1)}, s32[4]{0:T(128)}, u32[]{:S(2)}) copy-start(s32[4]{0:T(128)} %j_ref.1) | copy-start | bytes 52

commit v7 on v6

--- a/solution.py
+++ b/solution.py
@@ -40,9 +40,9 @@
 
 
 def kernel(
-    int_ref, a_ref, virt_ref, index_ref, pair_ref, occ_ref, i_ref, j_ref,
+    int_hbm, amp_hbm, virt_ref, index_hbm, pair_hbm, occ_ref, i_ref, j_ref,
     out_ref,
-    g_ref, g_rows, column_buf, gh0, gh1, spaced, moved, dbuf, arrived, ebuf, acc, zsend, zrecv, ysum, ygath,
+    int_ref, amp_ref, index_ref, pair_ref, load_sem, g_ref, g_rows, a_ref, column_buf, gh0, gh1, spaced, moved, dbuf, arrived, ebuf, acc, zsend, zrecv, ysum, ygath,
     own_sem, p0_send, p0_recv, p1_send, p1_recv, q0_send, q0_recv, q1_send, q1_recv,
     s0_send, s0_recv, s1_send, s1_recv, d_send, d_recv, z_send, z_recv, y_send, y_recv,
 ):
@@ -67,6 +67,15 @@
             src_ref=src, dst_ref=dst, send_sem=send, recv_sem=recv, device_id=device, device_id_type=MESH
         )
 
+    load_index = pltpu.make_async_copy(index_hbm, index_ref, load_sem.at[0])
+    load_int = pltpu.make_async_copy(int_hbm, int_ref, load_sem.at[1])
+    load_amp = pltpu.make_async_copy(amp_hbm, amp_ref, load_sem.at[2])
+    load_pair = pltpu.make_async_copy(pair_hbm, pair_ref, load_sem.at[3])
+    load_index.start()
+    load_int.start()
+    load_amp.start()
+    load_pair.start()
+
     barrier = pltpu.get_barrier_semaphore()
 
     def greet(device):
@@ -116,8 +125,10 @@
         return jnp.where(row == places, 1.0, 0.0).astype(BF16)
 
     p_all = onehot(place.astype(jnp.int32))
+    load_index.wait()
     valid, s_bj = own_label(5, 128)
     s_bj = jnp.bitwise_xor(s_bj, pick(irr_j, constant(6, 128)))
+    load_int.wait()
     for k in range(NK):
         for b in range(NA):
             g_rows[k, b * NJ:(b + 1) * NJ] = int_ref[k, b]
@@ -140,6 +151,13 @@
 
     each(1, 4, lambda o: p0(o).start())
     each(1, 4, lambda o: p1(o).start())
+
+    load_amp.wait()
+    for k in range(NK):
+        for i in range(NI):
+            first = (NI * k + i) * CPAD
+            a_ref[first + 16:first + CPAD] = jnp.zeros((8, NV), F32)
+            a_ref[first:first + NA] = amp_ref[i, :, k, :]
 
     a_high, a_low = halves(a_ref[...])
     for n in range(4):
@@ -244,6 +262,8 @@
     q1(1, 1).start()
     s1(0).start()
 
+    load_pair.wait()
+
     @pl.loop(0, 8)
     def _(n):
         row = lax.broadcasted_iota(jnp.int32, (NJ * CAP, GROUP), 0)
@@ -281,6 +301,11 @@
         d = (me + n) % BLK
         remote(moved.at[d], dbuf.at[d], d_send.at[d], d_recv.at[d], (d, mz)).wait_recv()
 
+    for o in (1, 0):
+        q0(o, 0).wait_recv()
+        r0(o).start()
+        q1(o, 0).wait_recv()
+        r1(o).start()
     each(1, BLK, d_wait)
     @pl.loop(0, BLK)
     def _(d):
@@ -326,11 +351,6 @@
         row = (cx + order(n)) % 4
         product(gh1[row], 4 + row)
 
-    for o in (1, 0):
-        q0(o, 0).wait_recv()
-        r0(o).start()
-        q1(o, 0).wait_recv()
-        r1(o).start()
     for o in (1, 0):
         q0(o, 1).wait_recv()
         s0(2 - o).start()
@@ -412,10 +432,6 @@
     for half in range(2):
         each(1, INT, lambda n: z_copy(n, half).wait_send())
         each(1, INT, lambda n: y_copy(n, half).wait_send())
-
-
-def pad_to(x, shape, value=0):
-    return jnp.pad(x, [(0, n - m) for n, m in zip(shape, x.shape)], constant_values=value)
 
 
 def index_tables():
@@ -451,20 +467,26 @@
 
 
 def per_device(amplitudes, integrals, occ_irrep, virt_irrep, i_batch, j_batch):
-    a_rows = pad_to(jnp.transpose(amplitudes, (2, 0, 1, 3)), (NK, NI, CPAD, NV)).reshape(NK * NI * CPAD, NV)
     ints = jnp.transpose(integrals, (0, 3, 2, 1))
     table, pairs = index_tables()
 
     vmem = pl.BlockSpec(memory_space=pltpu.VMEM)
+    hbm = pl.BlockSpec(memory_space=pltpu.HBM)
     dma = pltpu.SemaphoreType.DMA
     out = pl.pallas_call(
         kernel,
         out_shape=jax.ShapeDtypeStruct((ROWS, 256), F32),
-        in_specs=[vmem] * 5 + [pl.BlockSpec(memory_space=pltpu.SMEM)] * 3,
+        in_specs=[hbm, hbm, vmem, hbm, hbm] + [pl.BlockSpec(memory_space=pltpu.SMEM)] * 3,
         out_specs=vmem,
         scratch_shapes=[
+            pltpu.VMEM((NK, NA, NJ, NV), F32),
+            pltpu.VMEM((NI, NA, NK, NV), F32),
+            pltpu.VMEM((16, BLK * CPAD), jnp.int32),
+            pltpu.VMEM((8, 2, 384), jnp.int32),
+            dma((4,)),
             pltpu.VMEM((ROWS, NK * CAP), F32),
             pltpu.VMEM((NK, ROWS, NV), F32),
+            pltpu.VMEM((NI * NK * CPAD, NV), F32),
             pltpu.VMEM((8, GROUP, 1), jnp.int32),
             pltpu.VMEM((4, 2, 4, HALF, NK * CAP), F32),
             pltpu.VMEM((4, 2, 4, HALF, NK * CAP), F32),
@@ -483,10 +505,10 @@
             dma((2 * INT,)), dma((2 * INT,)), dma((2 * INT,)), dma((2 * INT,)),
         ],
         compiler_params=pltpu.CompilerParams(
-            collective_id=0, has_side_effects=True, vmem_limit_bytes=48 * 1024 * 1024
+            collective_id=0, has_side_effects=True, vmem_limit_bytes=66850000
         ),
     )(
-        ints, a_rows, virt_irrep.reshape(1, NV), jnp.asarray(table), jnp.asarray(pairs), occ_irrep, i_batch, j_batch
+        ints, amplitudes, virt_irrep.reshape(1, NV), jnp.asarray(table), jnp.asarray(pairs), occ_irrep, i_batch, j_batch
     )
     return out[:NI * NA, :NJ * NB].reshape(NI, NA, NJ, NB)
 

time: 69.5 us -> 71.6 us (1.030)
  Pallas kernels: 65.7 us -> 68.5 us
    pallas_call x1, Pallas kernels: 65.7 us -> 68.5 us  [per_device(): pl.pallas_call(kernel, out_shape=jax.ShapeDtypeStruct((ROWS, 256), F32),...]
    unnamed x15 -> x0, local copies, waits for them, and re-layouts: 2.53 us -> none
    reshape x1, local copies, waits for them, and re-layouts: 0.01 us -> 1.27 us  [per_device(): virt_irrep.reshape(1, NV)]
    reshape x1, local copies, waits for them, and re-layouts: 0.8 us -> 1.68 us  [per_device(): return out[:NI * NA, :NJ * NB].reshape(NI, NA, NJ, NB)]
where the time goes in v7:
time: 71.6 us; the launch traced here: 71.4 us
  Pallas kernels  68.5 us (96%)
  local copies, waits for them, and re-layouts  2.95 us (4%)
    pallas_call x1, Pallas kernels, per_device(): pl.pallas_call(kernel, out_shape=jax.ShapeDtypeStruct((ROWS, 256), F32),...  68.5 us
    reshape x1, local copies, waits for them, and re-layouts, per_device(): return out[:NI * NA, :NJ * NB].reshape(NI, NA, NJ, NB)  1.68 us

profile of v7, /device:TPU:1, one launch (start us, length us, event | category | flops | bytes accessed | tf_op | source)
XLA Modules:
  0.0 71.4 jit_solution(6784047799308160694)
XLA Ops:
  0.0 1.3 %reshape.6.virt_ref = s32[1,608]{1,0:T(1,128)} reshape(s32[608]{0:T(1024)} %param.11) | data formatting | bytes 4864 | tf_op jit(solution)/shard_map/reshape | solution.py:511
  1.3 68.5 %shard_map.82 = f32[80,256]{1,0:T(8,128)} custom-call(f32[4,19,4,608]{3,2,1,0:T(4,128)} %bitcast.2, f32[4,19,4,608]{3,2,1,0:T(4,128)} %amp_hbm.1, s32[1,608]{1,0:T(1,128)} %reshape.6.virt_ref, s32[16,768]{1,0:T(8,128)} %constant.4.clone.index_hbm, s32[8,2,384]{2,1,0:T(2,128)} %constant.5.clone.pair_hbm, s32[64]{0:T(128)} %occ_ref.1, s32[4]{0:T(128)} %i_ref.1, ...), custom_call_target="tpu_custom_call" | custom-call | tf_op jit(solution)/shard_map/pallas_call | solution.py:476
  69.7 1.7 %reshape.7 = f32[4,19,4,38]{3,2,1,0:T(4,128)} reshape(f32[76,152]{1,0:T(8,128)} %bitcast.3) | data formatting | bytes 92416 | tf_op jit(solution)/shard_map/reshape | solution.py:513

commit v8 on v6

--- a/solution.py
+++ b/solution.py
@@ -138,8 +138,9 @@
     def p1(o):
         return remote(g_ref.at[pl.ds(HALF, HALF)], gh1.at[cx, core, cy], p1_send.at[o], p1_recv.at[o], plane(cy + o, cx, core))
 
-    each(1, 4, lambda o: p0(o).start())
-    each(1, 4, lambda o: p1(o).start())
+    for o in (2, 1, 3):
+        p0(o).start()
+        p1(o).start()
 
     a_high, a_low = halves(a_ref[...])
     for n in range(4):
@@ -281,6 +282,11 @@
         d = (me + n) % BLK
         remote(moved.at[d], dbuf.at[d], d_send.at[d], d_recv.at[d], (d, mz)).wait_recv()
 
+    for o in (1, 0):
+        q0(o, 0).wait_recv()
+        r0(o).start()
+        q1(o, 0).wait_recv()
+        r1(o).start()
     each(1, BLK, d_wait)
     @pl.loop(0, BLK)
     def _(d):
@@ -326,11 +332,6 @@
         row = (cx + order(n)) % 4
         product(gh1[row], 4 + row)
 
-    for o in (1, 0):
-        q0(o, 0).wait_recv()
-        r0(o).start()
-        q1(o, 0).wait_recv()
-        r1(o).start()
     for o in (1, 0):
         q0(o, 1).wait_recv()
         s0(2 - o).start()

time: 69.5 us -> 70.9 us (1.020)
  Pallas kernels: 65.7 us -> 67.2 us
    pallas_call x1, Pallas kernels: 65.7 us -> 67.2 us  [per_device(): pl.pallas_call(kernel, out_shape=jax.ShapeDtypeStruct((ROWS, 256), F32),...]
where the time goes in v8:
time: 70.9 us; the launch traced here: 70.6 us
  Pallas kernels  67.2 us (95%)
  local copies, waits for them, and re-layouts  3.4 us (5%)
    pallas_call x1, Pallas kernels, per_device(): pl.pallas_call(kernel, out_shape=jax.ShapeDtypeStruct((ROWS, 256), F32),...  67.2 us
    unnamed x15, local copies, waits for them, and re-layouts  2.53 us

profile of v8, /device:TPU:1, one launch (start us, length us, event | category | flops | bytes accessed | tf_op | source)
XLA Modules:
  0.0 70.6 jit_solution(17517734164615650085)
XLA Ops:
  0.0 1.2 %copy.11 = f32[4,4,19,608]{3,2,1,0:T(8,128)S(1)} copy(f32[4,4,19,608]{3,0,2,1:T(4,128)} %bitcast.7) | data formatting | bytes 1478656
  1.2 0.0 copy-start.6
  1.2 0.0 copy-start
  1.2 0.0 copy-start.1
  1.2 0.0 copy-start.2
  1.3 0.1 pad.4.clone
  1.3 0.6 copy-done.6
  1.9 0.0 copy-start.3
  1.9 0.0 copy-start.4
  1.9 0.0 copy-start.5
  1.9 0.4 copy-done
  2.4 0.0 copy-done.1
  2.4 0.0 copy-done.2
  2.4 0.3 copy-done.3
  2.6 0.0 copy-done.4
  2.6 0.0 copy-done.5
  2.7 67.2 %shard_map.82 = f32[80,256]{1,0:T(8,128)S(1)} custom-call(f32[4,19,4,608]{3,2,1,0:T(4,128)S(1)} %bitcast.5, f32[384,608]{1,0:T(8,128)S(1)} %bitcast.4, s32[1,608]{1,0:T(1,128)S(1)} %reshape.10.virt_ref, s32[16,768]{1,0:T(8,128)S(1)} %copy-done.1, s32[8,2,384]{2,1,0:T(2,128)S(1)} %copy-done.2, s32[64]{0:T(128)S(1)} %copy-done.3, s32[4]{0:T(128)S(1)} %copy-done.4, ...), custom_call_target="tpu_custom_call" | custom-call | tf_op jit(solution)/shard_map/pallas_call | solution.py:461
  69.8 0.8 %reshape.11 = f32[4,19,4,38]{3,2,1,0:T(4,128)} reshape(f32[76,152]{1,0:T(8,128)S(1)} %bitcast.6) | data formatting | bytes 92416 | tf_op jit(solution)/shard_map/reshape | solution.py:492
  (1 shorter events, 0.0 us)
Async XLA Ops:
  1.2 0.7 copy-start.6
  1.2 1.1 %copy-start = (f32[4,608,4,19]{1,2,3,0:T(4,128)S(1)}, f32[4,608,4,19]{1,2,3,0:T(4,128)}, u32[]{:S(2)}) copy-start(f32[4,608,4,19]{1,2,3,0:T(4,128)} %param.9) | copy-start | bytes 2217988
  1.2 1.1 %copy-start.1 = (s32[16,768]{1,0:T(8,128)S(1)}, s32[16,768]{1,0:T(8,128)}, u32[]{:S(2)}) copy-start(s32[16,768]{1,0:T(8,128)} %constant.7.clone.index_ref) | copy-start | bytes 147460
  1.2 1.1 %copy-start.2 = (s32[8,2,384]{2,1,0:T(2,128)S(1)}, s32[8,2,384]{2,1,0:T(2,128)}, u32[]{:S(2)}) copy-start(s32[8,2,384]{2,1,0:T(2,128)} %constant.8.clone.pair_ref) | copy-start | bytes 73732
  1.9 0.7 %copy-start.3 = (s32[64]{0:T(128)S(1)}, s32[64]{0:T(128)}, u32[]{:S(2)}) copy-start(s32[64]{0:T(128)} %occ_ref.1) | copy-start | bytes 772
  1.9 0.7 %copy-start.4 = (s32[4]{0:T(128)S(1)}, s32[4]{0:T(128)}, u32[]{:S(2)}) copy-start(s32[4]{0:T(128)} %i_ref.1) | copy-start | bytes 52
  1.9 0.7 %copy-start.5 = (s32[4]{0:T(128)S(1)}, s32[4]{0:T(128)}, u32[]{:S(2)}) copy-start(s32[4]{0:T(128)} %j_ref.1) | copy-start | bytes 52

commit v9 on v6

--- a/solution.py
+++ b/solution.py
@@ -331,13 +331,15 @@
         r0(o).start()
         q1(o, 0).wait_recv()
         r1(o).start()
-    for o in (1, 0):
-        q0(o, 1).wait_recv()
-        s0(2 - o).start()
-        q1(o, 1).wait_recv()
-        s1(2 - o).start()
-
     def products(n, c):
+        @pl.when(n == 1)
+        def _():
+            for o in (1, 0):
+                q0(o, 1).wait_recv()
+                s0(2 - o).start()
+                q1(o, 1).wait_recv()
+                s1(2 - o).start()
+
         @pl.when(n == 3)
         def _():
             r0(0).wait_recv()

time: 69.5 us -> 69.5 us (level)
  no operation moved by 1% of the time
where the time goes in v9:
time: 69.5 us; the launch traced here: 69.2 us
  Pallas kernels  65.7 us (95%)
  local copies, waits for them, and re-layouts  3.4 us (5%)
    pallas_call x1, Pallas kernels, per_device(): pl.pallas_call(kernel, out_shape=jax.ShapeDtypeStruct((ROWS, 256), F32),...  65.7 us
    unnamed x15, local copies, waits for them, and re-layouts  2.53 us

profile of v9, /device:TPU:1, one launch (start us, length us, event | category | flops | bytes accessed | tf_op | source)
XLA Modules:
  0.0 69.2 jit_solution(9940148129994063619)
XLA Ops:
  0.0 1.2 %copy.11 = f32[4,4,19,608]{3,2,1,0:T(8,128)S(1)} copy(f32[4,4,19,608]{3,0,2,1:T(4,128)} %bitcast.7) | data formatting | bytes 1478656
  1.2 0.0 copy-start.6
  1.2 0.0 copy-start
  1.2 0.0 copy-start.1
  1.2 0.0 copy-start.2
  1.3 0.1 pad.4.clone
  1.3 0.6 copy-done.6
  1.9 0.0 copy-start.3
  1.9 0.0 copy-start.4
  1.9 0.0 copy-start.5
  1.9 0.4 copy-done
  2.4 0.0 copy-done.1
  2.4 0.0 copy-done.2
  2.4 0.3 copy-done.3
  2.6 0.0 copy-done.4
  2.6 0.0 copy-done.5
  2.7 65.7 %shard_map.82 = f32[80,256]{1,0:T(8,128)S(1)} custom-call(f32[4,19,4,608]{3,2,1,0:T(4,128)S(1)} %bitcast.5, f32[384,608]{1,0:T(8,128)S(1)} %bitcast.4, s32[1,608]{1,0:T(1,128)S(1)} %reshape.10.virt_ref, s32[16,768]{1,0:T(8,128)S(1)} %copy-done.1, s32[8,2,384]{2,1,0:T(2,128)S(1)} %copy-done.2, s32[64]{0:T(128)S(1)} %copy-done.3, s32[4]{0:T(128)S(1)} %copy-done.4, ...), custom_call_target="tpu_custom_call" | custom-call | tf_op jit(solution)/shard_map/pallas_call | solution.py:462
  68.4 0.8 %reshape.11 = f32[4,19,4,38]{3,2,1,0:T(4,128)} reshape(f32[76,152]{1,0:T(8,128)S(1)} %bitcast.6) | data formatting | bytes 92416 | tf_op jit(solution)/shard_map/reshape | solution.py:493
  (1 shorter events, 0.0 us)
Async XLA Ops:
  1.2 0.7 copy-start.6
  1.2 1.1 %copy-start = (f32[4,608,4,19]{1,2,3,0:T(4,128)S(1)}, f32[4,608,4,19]{1,2,3,0:T(4,128)}, u32[]{:S(2)}) copy-start(f32[4,608,4,19]{1,2,3,0:T(4,128)} %param.9) | copy-start | bytes 2217988
  1.2 1.1 %copy-start.1 = (s32[16,768]{1,0:T(8,128)S(1)}, s32[16,768]{1,0:T(8,128)}, u32[]{:S(2)}) copy-start(s32[16,768]{1,0:T(8,128)} %constant.7.clone.index_ref) | copy-start | bytes 147460
  1.2 1.1 %copy-start.2 = (s32[8,2,384]{2,1,0:T(2,128)S(1)}, s32[8,2,384]{2,1,0:T(2,128)}, u32[]{:S(2)}) copy-start(s32[8,2,384]{2,1,0:T(2,128)} %constant.8.clone.pair_ref) | copy-start | bytes 73732
  1.9 0.7 %copy-start.3 = (s32[64]{0:T(128)S(1)}, s32[64]{0:T(128)}, u32[]{:S(2)}) copy-start(s32[64]{0:T(128)} %occ_ref.1) | copy-start | bytes 772
  1.9 0.7 %copy-start.4 = (s32[4]{0:T(128)S(1)}, s32[4]{0:T(128)}, u32[]{:S(2)}) copy-start(s32[4]{0:T(128)} %i_ref.1) | copy-start | bytes 52
  1.9 0.7 %copy-start.5 = (s32[4]{0:T(128)S(1)}, s32[4]{0:T(128)}, u32[]{:S(2)}) copy-start(s32[4]{0:T(128)} %j_ref.1) | copy-start | bytes 52

commit v10 on v9

--- a/solution.py
+++ b/solution.py
@@ -334,11 +334,17 @@
     def products(n, c):
         @pl.when(n == 1)
         def _():
-            for o in (1, 0):
-                q0(o, 1).wait_recv()
-                s0(2 - o).start()
-                q1(o, 1).wait_recv()
-                s1(2 - o).start()
+            q0(1, 1).wait_recv()
+            s0(1).start()
+            q1(1, 1).wait_recv()
+            s1(1).start()
+
+        @pl.when(n == 2)
+        def _():
+            q0(0, 1).wait_recv()
+            s0(2).start()
+            q1(0, 1).wait_recv()
+            s1(2).start()
 
         @pl.when(n == 3)
         def _():

time: 69.5 us -> 70.5 us (1.014)
  the two profiles are of different devices: /device:TPU:1 before, /device:TPU:8 now
where the time goes in v10:
time: 70.5 us; the launch traced here: 70.3 us
  Pallas kernels  66.8 us (95%)
  local copies, waits for them, and re-layouts  3.4 us (5%)
    pallas_call x1, Pallas kernels, per_device(): pl.pallas_call(kernel, out_shape=jax.ShapeDtypeStruct((ROWS, 256), F32),...  66.8 us
    unnamed x15, local copies, waits for them, and re-layouts  2.53 us

profile of v10, /device:TPU:8, one launch (start us, length us, event | category | flops | bytes accessed | tf_op | source)
XLA Modules:
  0.0 70.3 jit_solution(14507335158489176044)
XLA Ops:
  0.0 1.2 %copy.11 = f32[4,4,19,608]{3,2,1,0:T(8,128)S(1)} copy(f32[4,4,19,608]{3,0,2,1:T(4,128)} %bitcast.7) | data formatting | bytes 1478656
  1.2 0.0 copy-start.6
  1.2 0.0 copy-start
  1.2 0.0 copy-start.1
  1.2 0.0 copy-start.2
  1.3 0.1 pad.4.clone
  1.3 0.6 copy-done.6
  1.9 0.0 copy-start.3
  1.9 0.0 copy-start.4
  1.9 0.0 copy-start.5
  1.9 0.4 copy-done
  2.4 0.0 copy-done.1
  2.4 0.0 copy-done.2
  2.4 0.3 copy-done.3
  2.6 0.0 copy-done.4
  2.6 0.0 copy-done.5
  2.7 66.8 %shard_map.82 = f32[80,256]{1,0:T(8,128)S(1)} custom-call(f32[4,19,4,608]{3,2,1,0:T(4,128)S(1)} %bitcast.5, f32[384,608]{1,0:T(8,128)S(1)} %bitcast.4, s32[1,608]{1,0:T(1,128)S(1)} %reshape.10.virt_ref, s32[16,768]{1,0:T(8,128)S(1)} %copy-done.1, s32[8,2,384]{2,1,0:T(2,128)S(1)} %copy-done.2, s32[64]{0:T(128)S(1)} %copy-done.3, s32[4]{0:T(128)S(1)} %copy-done.4, ...), custom_call_target="tpu_custom_call" | custom-call | tf_op jit(solution)/shard_map/pallas_call | solution.py:468
  69.5 0.8 %reshape.11 = f32[4,19,4,38]{3,2,1,0:T(4,128)} reshape(f32[76,152]{1,0:T(8,128)S(1)} %bitcast.6) | data formatting | bytes 92416 | tf_op jit(solution)/shard_map/reshape | solution.py:499
  (1 shorter events, 0.0 us)
Async XLA Ops:
  1.2 0.7 copy-start.6
  1.2 1.1 %copy-start = (f32[4,608,4,19]{1,2,3,0:T(4,128)S(1)}, f32[4,608,4,19]{1,2,3,0:T(4,128)}, u32[]{:S(2)}) copy-start(f32[4,608,4,19]{1,2,3,0:T(4,128)} %param.9) | copy-start | bytes 2217988
  1.2 1.1 %copy-start.1 = (s32[16,768]{1,0:T(8,128)S(1)}, s32[16,768]{1,0:T(8,128)}, u32[]{:S(2)}) copy-start(s32[16,768]{1,0:T(8,128)} %constant.7.clone.index_ref) | copy-start | bytes 147460
  1.2 1.1 %copy-start.2 = (s32[8,2,384]{2,1,0:T(2,128)S(1)}, s32[8,2,384]{2,1,0:T(2,128)}, u32[]{:S(2)}) copy-start(s32[8,2,384]{2,1,0:T(2,128)} %constant.8.clone.pair_ref) | copy-start | bytes 73732
  1.9 0.7 %copy-start.3 = (s32[64]{0:T(128)S(1)}, s32[64]{0:T(128)}, u32[]{:S(2)}) copy-start(s32[64]{0:T(128)} %occ_ref.1) | copy-start | bytes 772
  1.9 0.7 %copy-start.4 = (s32[4]{0:T(128)S(1)}, s32[4]{0:T(128)}, u32[]{:S(2)}) copy-start(s32[4]{0:T(128)} %i_ref.1) | copy-start | bytes 52
  1.9 0.7 %copy-start.5 = (s32[4]{0:T(128)S(1)}, s32[4]{0:T(128)}, u32[]{:S(2)}) copy-start(s32[4]{0:T(128)} %j_ref.1) | copy-start | bytes 52
